TPU v7x, 256 devices: a whole 4x4x8 slice. The times are simulated.
256 devices in a mesh: roll: 64 (over z, y_lo, x), tp: 4 (over y_hi, core).
Axes of the slice: x: 4, y: 4 (y_hi: 2, y_lo: 2; y = y_hi * 2 + y_lo), z: 8, core: 2. Of those that a mesh axis runs over, the one named last changes fastest.
Arguments:
- hidden_in: bfloat16 [8192, 5120], P('roll', 'tp'), may hold values from -480 to 480
- qkv_weight: bfloat16 [5120, 3584], P('roll', 'tp'), may hold values from -1 to 1
- sample_group: int32 [8192], P('roll'), may hold values from 0 to 127, as said below
- prefix_blocks: int32 [128], P('roll'), may hold values from 1 to 4, as said below
- prefix_kv: bfloat16 [128, 512, 1024], P('roll', None, 'tp'), may hold values from -24 to 24
- page_table: int32 [8192, 2], P('roll'), may hold values from 0 to 255, as said below
- suffix_pool: bfloat16 [16384, 16, 1024], P('roll', None, 'tp'), may hold values from -24 to 24
Outputs:
- attended: bfloat16 [8192, 2560], P('roll', 'tp')
Inputs may be any that keep to these rules, and one draw needn't show every extreme that they name: `sample_group`: on each index of roll the 128 entries name every group exactly once. `prefix_blocks`: some group has exactly 4 blocks. `page_table`: on each index of roll the entries are a permutation of 0 to 255.
All inputs are finite; a program needn't handle non-finite values.
Results may differ from a plain program's by a relative error of at most 0.0096.
Values may be sent and summed in bfloat16 or wider, within the bound.
A program may use at most 64 MiB of HBM per device.

v0:
```python
import math

import jax
import jax.numpy as jnp
from jax import lax
from jax.sharding import PartitionSpec as P

HEADS = 20
KV_HEADS = 4
HD = 128
BLOCK = 128
PAGE = 16
SPAGES = 2


MASKED = -1e30


def softmax_parts(scores):
    row_max = jnp.max(scores, axis=-1)
    exponent = jnp.exp(scores - row_max[..., None])
    row_sum = jnp.sum(exponent, axis=-1)
    return (exponent, row_max, row_sum)


def merge_parts(first_out, first_lse, second_out, second_lse):
    combined = jnp.logaddexp(first_lse, second_lse)
    mixed = (
        jnp.exp(first_lse - combined)[..., None] * first_out
        + jnp.exp(second_lse - combined)[..., None] * second_out
    )
    return mixed.astype(jnp.bfloat16)


def per_device(
    hidden_in, qkv_weight, sample_group, prefix_blocks, prefix_kv, page_table, suffix_pool
):
    whole = lax.all_gather(hidden_in, "tp", axis=1, tiled=True)
    row_count = whole.shape[0]
    kv_heads_dev = prefix_kv.shape[2] // (2 * HD)
    repeat = HEADS // KV_HEADS
    q_width = kv_heads_dev * repeat * HD
    head_count = kv_heads_dev * repeat
    owned_groups = prefix_kv.shape[0]
    roll_count = lax.axis_size("roll")
    per_group = row_count // (roll_count * owned_groups)
    owner_rows = roll_count * per_group
    prefix_span = prefix_kv.shape[1]
    score_scale = 1.0 / math.sqrt(HD)
    float_in = whole.astype(jnp.float32)
    normed = (
        float_in * lax.rsqrt(jnp.mean(float_in * float_in, axis=-1, keepdims=True) + 1e-06)
    ).astype(jnp.bfloat16)
    united_proj = jnp.dot(
        normed,
        lax.all_gather(qkv_weight, "roll", axis=0, tiled=True),
        preferred_element_type=jnp.float32,
    )
    united_proj = united_proj.astype(jnp.bfloat16).reshape(row_count, kv_heads_dev, repeat + 2, HD)
    queries = united_proj[:, :, :repeat]
    own_key = united_proj[:, :, repeat]
    own_value = united_proj[:, :, repeat + 1]
    sort_order = jnp.argsort(sample_group, stable=True)

    def sample_layout(arrived, width, dtype):
        return (
            jnp.zeros((row_count, width), dtype)
            .at[sort_order]
            .set(arrived.reshape(row_count, width))
        )

    page_rows = suffix_pool[page_table].reshape(row_count, SPAGES * PAGE, kv_heads_dev, 2, HD)
    key_rows = jnp.concatenate([page_rows[:, :, :, 0], own_key[:, None]], axis=1)
    value_rows = jnp.concatenate([page_rows[:, :, :, 1], own_value[:, None]], axis=1)
    scores = (
        jnp.einsum("sjrd,stjd->sjrt", queries, key_rows, preferred_element_type=jnp.float32)
        * score_scale
    )
    exponent, row_max, row_sum = softmax_parts(scores)
    weights = (exponent / row_sum[..., None]).astype(jnp.bfloat16)
    result = jnp.einsum("sjrt,stjd->sjrd", weights, value_rows, preferred_element_type=jnp.float32)
    local_out = result
    local_lse = row_max + jnp.log(row_sum)
    incoming = lax.all_to_all(
        queries.reshape(row_count, q_width)[sort_order].reshape(
            roll_count, owned_groups, per_group, q_width
        ),
        "roll",
        split_axis=0,
        concat_axis=2,
        tiled=True,
    )
    kv_cache = prefix_kv.reshape(owned_groups, prefix_span, kv_heads_dev, 2, HD)
    scores = (
        jnp.einsum(
            "gqjrd,gtjd->gqjrt",
            incoming.reshape(owned_groups, owner_rows, kv_heads_dev, repeat, HD),
            kv_cache[:, :, :, 0],
            preferred_element_type=jnp.float32,
        )
        * score_scale
    )
    live_mask = (jnp.arange(prefix_span)[None, :] < prefix_blocks[:, None] * BLOCK)[
        :, None, None, None, :
    ]
    scores = jnp.where(live_mask, scores, MASKED)
    row_max = jnp.max(scores, axis=-1)
    exponent = jnp.where(live_mask, jnp.exp(scores - row_max[..., None]), 0.0)
    row_sum = jnp.sum(exponent, axis=-1)
    weights = (exponent / row_sum[..., None]).astype(jnp.bfloat16)
    result = jnp.einsum(
        "gqjrt,gtjd->gqjrd", weights, kv_cache[:, :, :, 1], preferred_element_type=jnp.float32
    )
    result, result_lse = (result, row_max + jnp.log(row_sum))
    back_out = lax.all_to_all(
        result.reshape(1, owned_groups, owner_rows, q_width),
        "roll",
        split_axis=2,
        concat_axis=0,
        tiled=True,
    )
    back_lse = lax.all_to_all(
        result_lse.reshape(1, owned_groups, owner_rows, head_count),
        "roll",
        split_axis=2,
        concat_axis=0,
        tiled=True,
    )
    prefix_out = sample_layout(back_out, q_width, jnp.float32)
    prefix_lse = sample_layout(back_lse, head_count, jnp.float32)
    prefix_out, prefix_lse = (
        prefix_out.reshape(row_count, kv_heads_dev, repeat, HD),
        prefix_lse.reshape(row_count, kv_heads_dev, repeat),
    )
    return merge_parts(prefix_out, prefix_lse, local_out, local_lse).reshape(row_count, q_width)


def solution(mesh):
    in_specs = (
        P("roll", "tp"),
        P("roll", "tp"),
        P("roll"),
        P("roll"),
        P("roll", None, "tp"),
        P("roll", None),
        P("roll", None, "tp"),
    )
    out_specs = P("roll", "tp")
    return jax.shard_map(
        per_device, mesh=mesh, in_specs=in_specs, out_specs=out_specs, check_vma=False
    )
```

profile of v0, /device:TPU:8, one launch (start us, length us, event | category | flops | bytes accessed | tf_op | source)
XLA Modules:
  0.0 428.0 jit_solution(3843228985545048968)
XLA Ops:
  8.9 2.0 copy.137
  11.0 2.1 gather_fusion.1
  13.1 4.0 reshape.185
  17.1 2.5 sort.17
  19.7 7.5 %fusion.40 = (bf16[128,32,1,1,128]{4,3,1,0,2:T(2,128)(2,1)}, bf16[128,32,1,1,128]{4,3,1,0,2:T(2,128)(2,1)}) fusion(bf16[128,32,1,2,128]{4,3,1,0,2:T(2,128)(2,1)} %reshape.185), kind=kLoop, calls=%fused_computation.69 | loop fusion | bytes 4194304 | tf_op jit(solution)/shard_map/slice | solution.py:73
  27.3 8.7 %all-gather.3.cloned.1.call-done = bf16[128,5120]{1,0:T(8,128)(2,1)} async-done(((bf16[128,1280]{1,0:T(8,128)(2,1)}), bf16[128,5120]{1,0:T(8,128)(2,1)}) %all-gather.3.cloned.1.call-update) | async-done | bytes 1310736 | tf_op jit(solution)/shard_map/all_gather | solution.py:38
  36.0 1.8 fusion
  37.8 311.2 %all-gather.5.cloned.1.call-done = bf16[5120,896]{1,0:T(8,128)(2,1)} async-done(((bf16[80,896]{1,0:T(8,128)(2,1)}), bf16[5120,896]{1,0:T(8,128)(2,1)}) %all-gather.5.cloned.1.call-update) | async-done | bytes 9175056 | tf_op jit(solution)/shard_map/all_gather | solution.py:56
  348.9 5.9 %fusion.19 = bf16[128,896]{1,0:T(8,128)(2,1)} fusion(bf16[5120,896]{1,0:T(8,128)(2,1)} %all-gather.5.cloned.1.call-done, bf16[128,5120]{1,0:T(8,128)(2,1)S(1)} %copy-done.1, f32[128]{0:T(128)S(1)} %add_rsqrt_fusion), kind=kOutput, calls=%fused_computation.30 | convolution fusion | flops 1176485888 | bytes 10715648 | tf_op jit(solution)/shard_map/dot_general | solution.py:54
  354.8 1.1 copy.131
  357.8 11.7 %all-to-all-start = ((bf16[64,2,1,640]{3,1,2,0:T(2,128)(2,1)}), bf16[64,2,1,640]{3,1,2,0:T(2,128)(2,1)S(1)}, u32[]{:S(2)}, u32[]{:S(2)}) async-start(bf16[64,2,1,640]{3,1,2,0:T(2,128)(2,1)} %bitcast.2), calls=%async_computation | async-start | bytes 327680 | tf_op jit(solution)/shard_map/all_to_all | solution.py:84
  369.4 4.1 copy_bitcast_fusion
  373.5 6.5 %all-to-all-done = bf16[64,2,1,640]{3,1,2,0:T(2,128)(2,1)S(1)} async-done(((bf16[64,2,1,640]{3,1,2,0:T(2,128)(2,1)}), bf16[64,2,1,640]{3,1,2,0:T(2,128)(2,1)S(1)}, u32[]{:S(2)}, u32[]{:S(2)}) %all-to-all-start) | async-done | bytes 163872 | tf_op jit(solution)/shard_map/all_to_all | solution.py:84
  380.8 1.4 bitcast_reduce_fusion
  383.4 5.0 %all-to-all-start.1 = ((f32[1,2,64,5]{3,1,0,2:T(2,128)}), f32[1,2,64,5]{3,1,0,2:T(2,128)S(1)}, u32[]{:S(2)}, u32[]{:S(2)}) async-start(f32[1,2,64,5]{3,1,0,2:T(2,128)} %copy.140), calls=%async_computation.1 | async-start | bytes 131072 | tf_op jit(solution)/shard_map/all_to_all | solution.py:122
  388.4 1.5 convolution_bitcast_fusion
  390.1 1.0 reshape.235
  391.0 7.3 %all-to-all-done.1 = f32[1,2,64,5]{3,1,0,2:T(2,128)S(1)} async-done(((f32[1,2,64,5]{3,1,0,2:T(2,128)}), f32[1,2,64,5]{3,1,0,2:T(2,128)S(1)}, u32[]{:S(2)}, u32[]{:S(2)}) %all-to-all-start.1) | async-done | bytes 2592 | tf_op jit(solution)/shard_map/all_to_all | solution.py:122
  398.3 5.3 %all-to-all-start.2 = ((f32[1,2,64,640]{3,1,0,2:T(2,128)}), f32[1,2,64,640]{3,1,0,2:T(2,128)S(1)}, u32[]{:S(2)}, u32[]{:S(2)}) async-start(f32[1,2,64,640]{3,1,0,2:T(2,128)} %reshape.235), calls=%async_computation.2 | async-start | bytes 655360 | tf_op jit(solution)/shard_map/all_to_all | solution.py:115
  405.5 2.2 fusion.42
  410.1 5.5 %all-to-all-done.2 = f32[1,2,64,640]{3,1,0,2:T(2,128)S(1)} async-done(((f32[1,2,64,640]{3,1,0,2:T(2,128)}), f32[1,2,64,640]{3,1,0,2:T(2,128)S(1)}, u32[]{:S(2)}, u32[]{:S(2)}) %all-to-all-start.2) | async-done | bytes 327712 | tf_op jit(solution)/shard_map/all_to_all | solution.py:115
  415.8 1.1 scatter_custom_fusion.1
  417.1 1.0 copy.155
  418.1 2.0 fusion.18
  (53 shorter events, 12.2 us)
Async XLA Ops:
  6.5 4.5 %copy-start = (bf16[256,16,256]{2,1,0:T(8,128)(2,1)S(1)}, bf16[256,16,256]{2,1,0:T(8,128)(2,1)}, u32[]{:S(2)}) copy-start(bf16[256,16,256]{2,1,0:T(8,128)(2,1)} %param.13) | copy-start | bytes 6291460
  6.5 29.5 %all-gather.3.cloned.1.call-start = ((), (), s32[]{:S(2)}) async-start(), calls=%async_computation.3 | async-start | bytes 1638400 | tf_op jit(solution)/shard_map/all_gather | solution.py:38
  7.3 341.7 %all-gather.5.cloned.1.call-start = ((), (), s32[]{:S(2)}) async-start(), calls=%async_computation.4 | async-start | bytes 9318400 | tf_op jit(solution)/shard_map/all_gather | solution.py:56
  13.1 4.0 copy-start.5
  13.1 6.6 %copy-start.6 = (s32[2]{0:T(128)S(1)}, s32[2]{0:T(128)}, u32[]{:S(2)}) copy-start(s32[2]{0:T(128)} %param.10) | copy-start | bytes 28
  36.0 312.9 %copy-start.1 = (bf16[128,5120]{1,0:T(8,128)(2,1)S(1)}, bf16[128,5120]{1,0:T(8,128)(2,1)}, u32[]{:S(2)}) copy-start(bf16[128,5120]{1,0:T(8,128)(2,1)} %all-gather.3.cloned.1.call-done) | copy-start | bytes 3932164
  355.9 1.8 copy-start.4
  356.0 17.5 %copy-start.2 = (bf16[128,1,5,128]{0,3,2,1:T(8,128)(2,1)}, bf16[128,1,5,128]{0,3,2,1:T(8,128)(2,1)S(1)}, u32[]{:S(2)}) copy-start(bf16[128,1,5,128]{0,3,2,1:T(8,128)(2,1)S(1)} %slice.32) | copy-start | bytes 491524
  357.8 22.2 %all-to-all-start = ((bf16[64,2,1,640]{3,1,2,0:T(2,128)(2,1)}), bf16[64,2,1,640]{3,1,2,0:T(2,128)(2,1)S(1)}, u32[]{:S(2)}, u32[]{:S(2)}) async-start(bf16[64,2,1,640]{3,1,2,0:T(2,128)(2,1)} %bitcast.2), calls=%async_computation | async-start | bytes 327680 | tf_op jit(solution)/shard_map/all_to_all | solution.py:84
  383.4 14.9 %all-to-all-start.1 = ((f32[1,2,64,5]{3,1,0,2:T(2,128)}), f32[1,2,64,5]{3,1,0,2:T(2,128)S(1)}, u32[]{:S(2)}, u32[]{:S(2)}) async-start(f32[1,2,64,5]{3,1,0,2:T(2,128)} %copy.140), calls=%async_computation.1 | async-start | bytes 131072 | tf_op jit(solution)/shard_map/all_to_all | solution.py:122
  389.9 14.5 %copy-start.3 = (bf16[128,1,5,128]{0,3,2,1:T(8,128)(2,1)S(1)}, bf16[128,1,5,128]{0,3,2,1:T(8,128)(2,1)}, u32[]{:S(2)}) copy-start(bf16[128,1,5,128]{0,3,2,1:T(8,128)(2,1)} %copy-done.2) | copy-start | bytes 491524
  398.3 17.3 %all-to-all-start.2 = ((f32[1,2,64,640]{3,1,0,2:T(2,128)}), f32[1,2,64,640]{3,1,0,2:T(2,128)S(1)}, u32[]{:S(2)}, u32[]{:S(2)}) async-start(f32[1,2,64,640]{3,1,0,2:T(2,128)} %reshape.235), calls=%async_computation.2 | async-start | bytes 655360 | tf_op jit(solution)/shard_map/all_to_all | solution.py:115
Sparse Core Ops, SparseCore 0:
  9.2 26.7 all-gather.2
  37.8 311.1 all-gather.4
where the time goes:
time: 429 us; the launch traced here: 428 us
  waiting for transfers between devices  341 us (79%)
  local copies, waits for them, and re-layouts  33 us (8%)
  starting transfers between devices  21.9 us (5%)
  between operations  13.6 us (3%)
  matrix products  12.9 us (3%)
  other arithmetic  5.93 us (1%)
    all_gather x1, waiting for transfers between devices, per_device(): lax.all_gather(qkv_weight, 'roll', axis=0, tiled=True)  311 us
    all_to_all x1, starting transfers between devices, per_device(): lax.all_to_all(queries.reshape(row_count, q_width)[sort_order].reshape(ro...  11.7 us
    all_gather x1, waiting for transfers between devices, per_device(): whole = lax.all_gather(hidden_in, 'tp', axis=1, tiled=True)  8.75 us
  transfers between devices with their start and end apart: 5, of which 5 were waited for; matrix products, arithmetic and copies ran while one was open for 8% of the time, Pallas kernels for 0%

commit v1 on v0

--- a/solution.py
+++ b/solution.py
@@ -1,8 +1,11 @@
+import functools
 import math
 
 import jax
 import jax.numpy as jnp
 from jax import lax
+from jax.experimental import pallas as pl
+from jax.experimental.pallas import tpu as pltpu
 from jax.sharding import PartitionSpec as P
 
 HEADS = 20
@@ -11,6 +14,12 @@
 BLOCK = 128
 PAGE = 16
 SPAGES = 2
+D = 5120
+NX, NY, NZ = 4, 2, 8
+ROWS = 128
+SHARD = 80
+XC, ZC = 512, 384
+MESH = pl.DeviceIdType.MESH
 
 
 MASKED = -1e30
@@ -32,11 +41,299 @@
     return mixed.astype(jnp.bfloat16)
 
 
+class Place:
+    def __init__(self):
+        self.r = lax.axis_index("roll")
+        self.t = lax.axis_index("tp")
+        self.x = lax.rem(self.r, NX)
+        self.y = lax.rem(lax.div(self.r, NX), NY)
+        self.z = lax.div(self.r, NX * NY)
+        self.t1 = self.t + 1 - 2 * lax.rem(self.t, 2)
+        self.t2 = lax.rem(self.t + 2, 4)
+        self.t3 = lax.rem(self.t1 + 2, 4)
+        self.ty = 1 - self.y
+
+    def roll(self, z, y, x):
+        return (z * NY + y) * NX + x
+
+    def zn(self, k):
+        return lax.rem(self.z + k + NZ, NZ)
+
+    def xn(self, k):
+        return lax.rem(self.x + k + NX, NX)
+
+    def at_z(self, k):
+        return {"roll": self.roll(self.zn(k), self.y, self.x), "tp": self.t}
+
+    def at_x(self, k):
+        return {"roll": self.roll(self.z, self.y, self.xn(k)), "tp": self.t}
+
+    def other(self, flip_y, tp):
+        y = self.ty if flip_y else self.y
+        return {"roll": self.roll(self.z, y, self.x), "tp": tp}
+
+
+class Sends:
+    def __init__(self):
+        self.copies = []
+
+    def __call__(self, src, dst, send, recv, device):
+        copy = pltpu.make_async_remote_copy(
+            src_ref=src, dst_ref=dst, send_sem=send, recv_sem=recv,
+            device_id=device, device_id_type=MESH,
+        )
+        copy.start()
+        self.copies.append(copy)
+
+    def finish(self):
+        for copy in self.copies:
+            copy.wait_send()
+
+
+def arrived(ref, sem):
+    pltpu.make_async_copy(ref, ref, sem).wait()
+
+
+CHUNKS = ((0, 256), (256, 256), (512, 256), (768, 128))
+
+
+def project_kernel(
+    hp, w, out,
+    wx, wz, ab, nb, ssq_s, ssq_r, cs, cr,
+    s_ss, r_ss, s_a, r_a, s_b, r_b, s_c, r_c,
+    s_xz, r_xz, s_zx, r_zx, s_xx, r_xx, s_zz, r_zz,
+):
+    me = Place()
+    send = Sends()
+    x, y, z, t = me.x, me.y, me.z, me.t
+    barrier = pltpu.get_barrier_semaphore()
+    peers = [
+        me.at_z(1), me.at_z(-1), me.at_x(1), me.at_x(-1),
+        me.other(True, t), me.other(False, me.t2), me.other(True, me.t2),
+        me.other(False, me.t1), me.other(False, me.t3),
+    ]
+    for peer in peers:
+        pl.semaphore_signal(barrier, inc=1, device_id=peer, device_id_type=MESH)
+
+    wx[z, x] = w[:, :XC]
+    wz[z, x] = w[:, XC:]
+    total = jnp.zeros((ROWS, 1), jnp.float32)
+    for side in range(2):
+        part = hp[side].astype(jnp.float32)
+        total += jnp.sum(part * part, axis=-1, keepdims=True)
+    flat = jnp.broadcast_to(total, (ROWS, ROWS)).T[:8]
+    ssq_s[...] = flat
+    pl.semaphore_wait(barrier, len(peers))
+
+    for k, tp in ((1, me.t1), (2, me.t2), (3, me.t3)):
+        send(ssq_s, ssq_r.at[k], s_ss.at[k], r_ss.at[k], me.other(False, tp))
+
+    XH = XC // 2
+    ZH = 256
+    full_x, half_x = pl.ds(0, XC), (pl.ds(0, XH), pl.ds(XH, XC - XH))
+    full_z, half_z = pl.ds(0, ZC), (pl.ds(0, ZH), pl.ds(ZH, ZC - ZH))
+
+    def xz_send(step, way):
+        sign = 1 - 2 * way
+        cols = full_x if step < 4 else half_x[way]
+        ref = wx.at[me.zn(-sign * (step - 1)), x, :, cols]
+        i = way * 4 + step - 1
+        send(ref, ref, s_xz.at[i], r_xz.at[i], me.at_z(sign))
+
+    def xz_wait(step, way):
+        sign = 1 - 2 * way
+        cols = full_x if step < 4 else half_x[way]
+        arrived(wx.at[me.zn(-sign * step), x, :, cols], r_xz.at[way * 4 + step - 1])
+
+    def xx_send(d, step, way):
+        sign = 1 - 2 * way
+        cols = full_x if step == 1 else half_x[way]
+        ref = wx.at[me.zn(d), me.xn(-sign * (step - 1)), :, cols]
+        i = way * 2 + step - 1
+        send(ref, ref, s_xx.at[d, i], r_xx.at[d, i], me.at_x(sign))
+
+    def xx_wait(d, step, way):
+        sign = 1 - 2 * way
+        cols = full_x if step == 1 else half_x[way]
+        arrived(wx.at[me.zn(d), me.xn(-sign * step), :, cols], r_xx.at[d, way * 2 + step - 1])
+
+    def zx_send(step, way):
+        sign = 1 - 2 * way
+        cols = full_z if step == 1 else half_z[way]
+        ref = wz.at[z, me.xn(-sign * (step - 1)), :, cols]
+        i = way * 2 + step - 1
+        send(ref, ref, s_zx.at[i], r_zx.at[i], me.at_x(sign))
+
+    def zx_wait(step, way):
+        sign = 1 - 2 * way
+        cols = full_z if step == 1 else half_z[way]
+        arrived(wz.at[z, me.xn(-sign * step), :, cols], r_zx.at[way * 2 + step - 1])
+
+    def zz_send(j, step, way):
+        sign = 1 - 2 * way
+        cols = full_z if step < 4 else half_z[way]
+        ref = wz.at[me.zn(-sign * (step - 1)), me.xn(j), :, cols]
+        i = way * 4 + step - 1
+        send(ref, ref, s_zz.at[j, i], r_zz.at[j, i], me.at_z(sign))
+
+    def zz_wait(j, step, way):
+        sign = 1 - 2 * way
+        cols = full_z if step < 4 else half_z[way]
+        arrived(wz.at[me.zn(-sign * step), me.xn(j), :, cols], r_zz.at[j, way * 4 + step - 1])
+
+    both = (0, 1)
+    for way in both:
+        xz_send(1, way)
+        zx_send(1, way)
+    for way in both:
+        xx_send(0, 1, way)
+        zz_send(0, 1, way)
+
+    ssum = flat
+    for k in (1, 2, 3):
+        arrived(ssq_r.at[k], r_ss.at[k])
+        ssum += ssq_r[k]
+    scale = lax.rsqrt(ssum / D + 1e-06)
+    scale = jnp.broadcast_to(scale[:1], (ROWS, ROWS)).T
+    for side in range(2):
+        for b in range(5):
+            cols = slice(b * 128, b * 128 + 128)
+            nb[side, :, cols] = (hp[side, :, cols].astype(jnp.float32) * scale).astype(jnp.bfloat16)
+    ab[t, y] = nb[y]
+    send(nb.at[me.ty], ab.at[t, y], s_a.at[0], r_a.at[0], me.other(True, t))
+    send(nb.at[y], ab.at[t, y], s_a.at[1], r_a.at[1], me.other(False, me.t2))
+    send(nb.at[me.ty], ab.at[t, y], s_a.at[2], r_a.at[2], me.other(True, me.t2))
+    sibling = me.other(False, me.t1)
+    send(nb.at[y], ab.at[t, y], s_b.at[3], r_b.at[3], sibling)
+
+    def x_first():
+        for way in both:
+            zx_wait(1, way)
+            zx_send(2, way)
+        for j in (3, 1):
+            for way in both:
+                zz_send(j, 1, way)
+
+    def xz_round(step):
+        for way in both:
+            xz_wait(step, way)
+            if step < 4:
+                xz_send(step + 1, way)
+        if step < 4:
+            for d in (NZ - step, step):
+                for way in both:
+                    xx_send(d, 1, way)
+        else:
+            for way in both:
+                xx_send(4, 1, way)
+
+    def zz_round(j, step):
+        for way in both:
+            zz_wait(j, step, way)
+            if step < 4:
+                zz_send(j, step + 1, way)
+
+    def xx_round(d):
+        for way in both:
+            xx_wait(d, 1, way)
+            xx_send(d, 2, way)
+
+    x_first()
+    xz_round(1)
+    for way in both:
+        zx_wait(2, way)
+    for way in both:
+        zz_send(2, 1, way)
+    xz_round(2)
+    xx_round(0)
+    zz_round(0, 1)
+    for i, (tp, yy) in enumerate(((t, me.ty), (me.t2, y), (me.t2, me.ty))):
+        arrived(ab.at[tp, yy], r_a.at[i])
+        send(ab.at[tp, yy], ab.at[tp, yy], s_b.at[i], r_b.at[i], sibling)
+    xz_round(3)
+    zz_round(3, 1)
+    zz_round(1, 1)
+    xx_round(7)
+    xx_round(1)
+    xz_round(4)
+    zz_round(2, 1)
+    zz_round(0, 2)
+    xx_round(6)
+    xx_round(2)
+    zz_round(3, 2)
+    zz_round(1, 2)
+    zz_round(2, 2)
+    xx_round(5)
+    xx_round(3)
+    zz_round(0, 3)
+    zz_round(3, 3)
+    zz_round(1, 3)
+    zz_round(2, 3)
+    xx_round(4)
+    for i, (tp, yy) in enumerate(
+        ((me.t1, me.ty), (me.t3, y), (me.t3, me.ty), (me.t1, y))
+    ):
+        arrived(ab.at[tp, yy], r_b.at[i])
+    for d in range(NZ):
+        for way in both:
+            xx_wait(d, 2, way)
+    for j in range(NX):
+        zz_round(j, 4)
+
+    partner = me.other(True, t)
+    for i, (start, width) in enumerate(CHUNKS):
+        src, at = (wx, start) if start < XC else (wz, start - XC)
+        acc = jnp.zeros((2 * ROWS, width), jnp.float32)
+        for tp in range(4):
+            acc += jnp.dot(
+                ab[tp].reshape(2 * ROWS, 640),
+                src[2 * tp : 2 * tp + 2, :, :, at : at + width].reshape(640, width),
+                preferred_element_type=jnp.float32,
+            )
+        cs[i, :, :, :width] = acc.reshape(2, ROWS, width)
+        send(
+            cs.at[i, me.ty, :, pl.ds(0, width)], cr.at[i, :, pl.ds(0, width)],
+            s_c.at[i], r_c.at[i], partner,
+        )
+    for i, (start, width) in enumerate(CHUNKS):
+        arrived(cr.at[i, :, pl.ds(0, width)], r_c.at[i])
+        out[:, start : start + width] = (cs[i, y, :, :width] + cr[i, :, :width]).astype(jnp.bfloat16)
+    send.finish()
+
+
+def project(hidden_in, qkv_weight):
+    hp = hidden_in.reshape(ROWS, 2, 2, 320).transpose(2, 0, 1, 3).reshape(2, ROWS, 640)
+    dma = pltpu.SemaphoreType.DMA
+    vmem = pl.BlockSpec(memory_space=pltpu.VMEM)
+    sems = []
+    for shape in ((4,), (3,), (4,), (4,), (8,), (4,), (8, 4), (4, 8)):
+        sems += [dma(shape), dma(shape)]
+    return pl.pallas_call(
+        project_kernel,
+        out_shape=jax.ShapeDtypeStruct((ROWS, XC + ZC), jnp.bfloat16),
+        in_specs=[vmem, vmem],
+        out_specs=vmem,
+        scratch_shapes=[
+            pltpu.VMEM((NZ, NX, SHARD, XC), jnp.bfloat16),
+            pltpu.VMEM((NZ, NX, SHARD, ZC), jnp.bfloat16),
+            pltpu.VMEM((4, 2, ROWS, 640), jnp.bfloat16),
+            pltpu.VMEM((2, ROWS, 640), jnp.bfloat16),
+            pltpu.VMEM((8, ROWS), jnp.float32),
+            pltpu.VMEM((4, 8, ROWS), jnp.float32),
+            pltpu.VMEM((4, 2, ROWS, 256), jnp.float32),
+            pltpu.VMEM((4, ROWS, 256), jnp.float32),
+            *sems,
+        ],
+        compiler_params=pltpu.CompilerParams(
+            collective_id=0, has_side_effects=True, vmem_limit_bytes=40 * 1024 * 1024
+        ),
+    )(hp, qkv_weight)
+
+
 def per_device(
     hidden_in, qkv_weight, sample_group, prefix_blocks, prefix_kv, page_table, suffix_pool
 ):
-    whole = lax.all_gather(hidden_in, "tp", axis=1, tiled=True)
-    row_count = whole.shape[0]
+    row_count = hidden_in.shape[0]
     kv_heads_dev = prefix_kv.shape[2] // (2 * HD)
     repeat = HEADS // KV_HEADS
     q_width = kv_heads_dev * repeat * HD
@@ -47,15 +344,7 @@
     owner_rows = roll_count * per_group
     prefix_span = prefix_kv.shape[1]
     score_scale = 1.0 / math.sqrt(HD)
-    float_in = whole.astype(jnp.float32)
-    normed = (
-        float_in * lax.rsqrt(jnp.mean(float_in * float_in, axis=-1, keepdims=True) + 1e-06)
-    ).astype(jnp.bfloat16)
-    united_proj = jnp.dot(
-        normed,
-        lax.all_gather(qkv_weight, "roll", axis=0, tiled=True),
-        preferred_element_type=jnp.float32,
-    )
+    united_proj = project(hidden_in, qkv_weight)
     united_proj = united_proj.astype(jnp.bfloat16).reshape(row_count, kv_heads_dev, repeat + 2, HD)
     queries = united_proj[:, :, :repeat]
     own_key = united_proj[:, :, repeat]

time: 429 us -> 131 us (0.31)
  waiting for transfers between devices: 341 us -> 12.7 us
  Pallas kernels: 0 us -> 50.5 us
  between operations: 13.6 us -> 0.27 us
  matrix products: 12.9 us -> 7.06 us
    all_gather x2 -> x0, waiting for transfers between devices: 320 us -> none  [the longest x1 311 us: per_device(): lax.all_gather(qkv_weight, 'roll', axis=0, tiled=True)]
    pallas_call x0 -> x1, Pallas kernels: none -> 50.5 us  [project(): pl.pallas_call(project_kernel, out_shape=jax.ShapeDtypeStruct((ROWS, XC +...]
    all_to_all x1, waiting for transfers between devices: 6.48 us -> 0.01 us  [per_device(): lax.all_to_all(queries.reshape(row_count, q_width)[sort_order].reshape(ro...]
    all_to_all x1, starting transfers between devices: 4.97 us -> 11.2 us  [per_device(): lax.all_to_all(result_lse.reshape(1, owned_groups, owner_rows, head_count...]
    dot_general x1 -> x0, matrix products: 5.87 us -> none  [per_device(): jnp.dot(normed, lax.all_gather(qkv_weight, 'roll', axis=0, tiled=True), p...]
  transfers between devices with their start and end apart: 5 -> 3, of which waited for: 5 -> 2; matrix products, arithmetic and copies ran while one was open for 8% -> 21% of each run, Pallas kernels for 0% -> 0%
where the time goes in v1:
time: 131 us
  Pallas kernels  50.5 us (39%)
  local copies, waits for them, and re-layouts  32.5 us (25%)
  starting transfers between devices  24.3 us (19%)
  waiting for transfers between devices  12.7 us (10%)
  matrix products  7.06 us (5%)
  other arithmetic  3.49 us (3%)
    pallas_call x1, Pallas kernels, project(): pl.pallas_call(project_kernel, out_shape=jax.ShapeDtypeStruct((ROWS, XC +...  50.5 us
    all_to_all x1, starting transfers between devices, per_device(): lax.all_to_all(result_lse.reshape(1, owned_groups, owner_rows, head_count...  11.2 us
    all_to_all x1, starting transfers between devices, per_device(): lax.all_to_all(queries.reshape(row_count, q_width)[sort_order].reshape(ro...  7.63 us
    slice x1, local copies, waits for them, and re-layouts, per_device(): page_rows[:, :, :, 0]  7.48 us
    all_to_all x1, waiting for transfers between devices, per_device(): lax.all_to_all(result_lse.reshape(1, owned_groups, owner_rows, head_count...  7.19 us
    all_to_all x1, waiting for transfers between devices, per_device(): lax.all_to_all(result.reshape(1, owned_groups, owner_rows, q_width), 'rol...  5.49 us
    all_to_all x1, starting transfers between devices, per_device(): lax.all_to_all(result.reshape(1, owned_groups, owner_rows, q_width), 'rol...  5.48 us
    squeeze x1, local copies, waits for them, and re-layouts, per_device(): page_rows[:, :, :, 1]  4.05 us
  transfers between devices with their start and end apart: 3, of which 2 were waited for; matrix products, arithmetic and copies ran while one was open for 21% of the time, Pallas kernels for 0%

profile of v1, /device:TPU:8, one launch (start us, length us, event | category | flops | bytes accessed | tf_op | source)
XLA Modules:
  0.0 130.8 jit_solution(3892807512936188910)
XLA Ops:
  0.0 1.3 %copy.147 = bf16[128,1280]{0,1:T(8,128)(2,1)S(1)} copy(bf16[128,1280]{1,0:T(8,128)(2,1)} %param.7) | data formatting | bytes 655360 | tf_op args[0]
  1.6 50.5 %shard_map.73 = bf16[128,896]{1,0:T(8,128)(2,1)S(1)} custom-call(bf16[2,128,640]{2,1,0:T(8,128)(2,1)S(1)} %copy.149.hp, bf16[80,896]{1,0:T(8,128)(2,1)S(1)} %copy-done.1), custom_call_target="tpu_custom_call" | custom-call | tf_op jit(solution)/shard_map/pallas_call | solution.py:311
  52.4 2.5 %sort.17 = (s32[128]{0:T(128)}, s32[128]{0:T(128)S(1)}) sort(s32[128]{0:T(128)S(1)} %copy-done.7, s32[128]{0:T(128)S(1)} %iota.11), dimensions={0}, to_apply=%region_0.0 | sort | flops 896 | bytes 2048 | tf_op jit(solution)/shard_map/jit(argsort)/sort | solution.py:352
  55.1 0.9 gather_fusion
  56.7 7.6 %all-to-all-start = ((bf16[64,2,1,640]{3,1,2,0:T(2,128)(2,1)}), bf16[64,2,1,640]{3,1,2,0:T(2,128)(2,1)S(1)}, u32[]{:S(2)}, u32[]{:S(2)}) async-start(bf16[64,2,1,640]{3,1,2,0:T(2,128)(2,1)} %bitcast.5), calls=%async_computation | async-start | bytes 327680 | tf_op jit(solution)/shard_map/all_to_all | solution.py:373
  64.7 2.1 %gather_fusion.1 = bf16[256,16,256]{2,1,0:T(8,128)(2,1)} fusion(bf16[256,16,256]{2,1,0:T(8,128)(2,1)S(1)} %copy-done, s32[1024]{0:T(1024)S(1)} %pad_clamp_fusion), kind=kCustom, calls=%fused_computation.1 | custom fusion | bytes 4195328 | tf_op jit(solution)/shard_map/gather | solution.py:361
  66.8 4.0 %reshape.185 = bf16[128,32,1,2,128]{4,3,1,0,2:T(2,128)(2,1)} reshape(bf16[256,16,256]{2,1,0:T(8,128)(2,1)} %gather_fusion.1) | data formatting | bytes 4194304 | tf_op jit(solution)/shard_map/reshape | solution.py:361
  70.8 7.5 %fusion.32 = (bf16[128,32,1,1,128]{4,3,1,0,2:T(2,128)(2,1)}, bf16[128,32,1,1,128]{4,3,1,0,2:T(2,128)(2,1)}) fusion(bf16[128,32,1,2,128]{4,3,1,0,2:T(2,128)(2,1)} %reshape.185), kind=kLoop, calls=%fused_computation.61 | loop fusion | bytes 4194304 | tf_op jit(solution)/shard_map/slice | solution.py:362
  78.2 1.0 copy.156
  79.3 4.0 %copy_bitcast_fusion = (bf16[128,32,1,128]{3,1,0,2:T(8,128)(2,1)}, bf16[128,32,1,128]{3,1,0,2:T(8,128)(2,1)}) fusion(bf16[128,32,1,1,128]{4,3,1,0,2:T(2,128)(2,1)} %get-tuple-element.8, bf16[128,32,1,1,128]{4,3,1,0,2:T(2,128)(2,1)} %get-tuple-element.7), kind=kLoop, calls=%fused_computation.26 | loop fusion | bytes 4194304 | tf_op jit(solution)/shard_map/squeeze | solution.py:363
  84.2 1.4 %bitcast_reduce_fusion = (f32[2,64,5]{1,2,0:T(8,128)S(1)}, f32[2,1,512,64,5]{2,3,4,0,1:T(8,128)S(1)}) fusion(bf16[2,512,1,2,128]{1,4,3,0,2:T(8,128)(2,1)} %bitcast.106, bf16[2,64,5,128]{3,2,0,1:T(8,128)(2,1)} %reshape.234, pred[2,512]{1,0:T(4,128)(4,1)S(1)} %iota_compare_fusion), kind=kOutput, calls=%fused_computation.15 | convolution fusion | flops 84868480 | bytes 1838592 | tf_op jit(solution)/shard_map/gqjrd,gtjd->gqjrt/dot_general | solution.py:384
  86.8 11.2 %all-to-all-start.1 = ((f32[1,2,64,5]{3,1,0,2:T(2,128)}), f32[1,2,64,5]{3,1,0,2:T(2,128)S(1)}, u32[]{:S(2)}, u32[]{:S(2)}) async-start(f32[1,2,64,5]{3,1,0,2:T(2,128)} %copy.159), calls=%async_computation.1 | async-start | bytes 131072 | tf_op jit(solution)/shard_map/all_to_all | solution.py:411
  98.0 1.5 %convolution_bitcast_fusion = f32[2,64,1,5,128]{4,1,3,0,2:T(8,128)S(1)} fusion(f32[2,1,512,64,5]{2,3,4,0,1:T(8,128)S(1)} %get-tuple-element.14, f32[2,64,5]{1,2,0:T(8,128)S(1)} %fusion.14, f32[2,64,5]{1,2,0:T(8,128)S(1)} %get-tuple-element.13, pred[2,512]{1,0:T(4,128)(4,1)S(1)} %iota_compare_fusion, bf16[2,512,1,2,128]{1,4,3,0,2:T(8,128)(2,1)} %bitcast.107), kind=kOutput, calls=%fused_computation.24 | convolution fusion | flops 85196800 | bytes 1906688 | tf_op jit(solution)/shard_map/gqjrt,gtjd->gqjrd/dot_general | solution.py:400
  99.7 0.9 reshape.235
  100.6 7.2 %all-to-all-done.1 = f32[1,2,64,5]{3,1,0,2:T(2,128)S(1)} async-done(((f32[1,2,64,5]{3,1,0,2:T(2,128)}), f32[1,2,64,5]{3,1,0,2:T(2,128)S(1)}, u32[]{:S(2)}, u32[]{:S(2)}) %all-to-all-start.1) | async-done | bytes 2592 | tf_op jit(solution)/shard_map/all_to_all | solution.py:411
  107.8 5.5 %all-to-all-start.2 = ((f32[1,2,64,640]{3,1,0,2:T(2,128)}), f32[1,2,64,640]{3,1,0,2:T(2,128)S(1)}, u32[]{:S(2)}, u32[]{:S(2)}) async-start(f32[1,2,64,640]{3,1,0,2:T(2,128)} %reshape.235), calls=%async_computation.2 | async-start | bytes 655360 | tf_op jit(solution)/shard_map/all_to_all | solution.py:404
  114.1 0.9 copy.186
  115.2 2.2 %fusion.34 = (f32[128,5]{1,0:T(8,128)S(1)}, f32[128,5,33]{2,1,0:T(8,128)S(1)}) fusion(bf16[128,1,1,128]{3,1,0,2:T(2,128)(2,1)S(1)} %copy.189, bf16[128,32,1,128]{3,1,0,2:T(8,128)(2,1)} %get-tuple-element.18, bf16[128,1,5,128]{3,2,0,1:T(8,128)(2,1)} %copy.186), kind=kOutput, calls=%fused_computation.63 | convolution fusion | flops 7611008 | bytes 1332224 | tf_op jit(solution)/shard_map/sjrd,stjd->sjrt/dot_general | solution.py:365
  117.9 0.9 scatter_custom_fusion
  119.8 5.5 %all-to-all-done.2 = f32[1,2,64,640]{3,1,0,2:T(2,128)S(1)} async-done(((f32[1,2,64,640]{3,1,0,2:T(2,128)}), f32[1,2,64,640]{3,1,0,2:T(2,128)S(1)}, u32[]{:S(2)}, u32[]{:S(2)}) %all-to-all-start.2) | async-done | bytes 327712 | tf_op jit(solution)/shard_map/all_to_all | solution.py:404
  125.5 1.1 scatter_custom_fusion.1
  126.8 1.0 copy.174
  127.8 2.0 %fusion.13 = bf16[128,5,128]{2,1,0:T(8,128)(2,1)S(1)} fusion(bf16[128,1,1,128]{3,1,0,2:T(2,128)(2,1)S(1)} %copy.192, bf16[128,32,1,128]{3,1,0,2:T(8,128)(2,1)} %get-tuple-element.17, f32[128,5,128]{2,1,0:T(8,128)} %copy.174, f32[128,5,33]{2,1,0:T(8,128)S(1)} %get-tuple-element.16, f32[128,5]{1,0:T(8,128)S(1)} %fusion.17, f32[128,5]{1,0:T(8,128)S(1)} %copy.175, ...), kind=kOutput, calls=%fused_computation.23 | convolution fusion | flops 7960448 | bytes 1667584 | tf_op jit(solution)/shard_map/sjrt,stjd->sjrd/dot_general | solution.py:370
  130.0 0.8 copy.179
  (52 shorter events, 7.0 us)
Async XLA Ops:
  0.0 64.7 %copy-start = (bf16[256,16,256]{2,1,0:T(8,128)(2,1)S(1)}, bf16[256,16,256]{2,1,0:T(8,128)(2,1)}, u32[]{:S(2)}) copy-start(bf16[256,16,256]{2,1,0:T(8,128)(2,1)} %param.13) | copy-start | bytes 6291460
  0.0 1.6 %copy-start.1 = (bf16[80,896]{1,0:T(8,128)(2,1)S(1)}, bf16[80,896]{1,0:T(8,128)(2,1)}, u32[]{:S(2)}) copy-start(bf16[80,896]{1,0:T(8,128)(2,1)} %w.1) | copy-start | bytes 430084
  1.3 51.0 %copy-start.7 = (s32[128]{0:T(128)S(1)}, s32[128]{0:T(128)}, u32[]{:S(2)}) copy-start(s32[128]{0:T(128)} %param.9) | copy-start | bytes 1540
  52.3 4.4 %copy-start.4 = (bf16[128,896]{0,1:T(8,128)(2,1)}, bf16[128,896]{0,1:T(8,128)(2,1)S(1)}, u32[]{:S(2)}) copy-start(bf16[128,896]{0,1:T(8,128)(2,1)S(1)} %copy.150) | copy-start | bytes 688132
  54.9 11.9 %copy-start.2 = (bf16[128,1,5,128]{0,3,2,1:T(8,128)(2,1)}, bf16[128,1,5,128]{0,3,2,1:T(8,128)(2,1)S(1)}, u32[]{:S(2)}) copy-start(bf16[128,1,5,128]{0,3,2,1:T(8,128)(2,1)S(1)} %slice.32) | copy-start | bytes 491524
  54.9 9.4 %copy-start.6 = (s32[128,2]{0,1:T(2,128)S(1)}, s32[128,2]{0,1:T(2,128)}, u32[]{:S(2)}) copy-start(s32[128,2]{0,1:T(2,128)} %param.12) | copy-start | bytes 3076
  56.7 26.7 %all-to-all-start = ((bf16[64,2,1,640]{3,1,2,0:T(2,128)(2,1)}), bf16[64,2,1,640]{3,1,2,0:T(2,128)(2,1)S(1)}, u32[]{:S(2)}, u32[]{:S(2)}) async-start(bf16[64,2,1,640]{3,1,2,0:T(2,128)(2,1)} %bitcast.5), calls=%async_computation | async-start | bytes 327680 | tf_op jit(solution)/shard_map/all_to_all | solution.py:373
  70.8 7.5 %copy-start.5 = (bf16[2,512,256]{2,1,0:T(8,128)(2,1)S(1)}, bf16[2,512,256]{2,1,0:T(8,128)(2,1)}, u32[]{:S(2)}) copy-start(bf16[2,512,256]{2,1,0:T(8,128)(2,1)} %param.11) | copy-start | bytes 1572868
  70.8 8.5 %copy-start.8 = (s32[2]{0:T(128)S(1)}, s32[2]{0:T(128)}, u32[]{:S(2)}) copy-start(s32[2]{0:T(128)} %param.10) | copy-start | bytes 28
  86.8 21.0 %all-to-all-start.1 = ((f32[1,2,64,5]{3,1,0,2:T(2,128)}), f32[1,2,64,5]{3,1,0,2:T(2,128)S(1)}, u32[]{:S(2)}, u32[]{:S(2)}) async-start(f32[1,2,64,5]{3,1,0,2:T(2,128)} %copy.159), calls=%async_computation.1 | async-start | bytes 131072 | tf_op jit(solution)/shard_map/all_to_all | solution.py:411
  99.5 14.6 %copy-start.3 = (bf16[128,1,5,128]{0,3,2,1:T(8,128)(2,1)S(1)}, bf16[128,1,5,128]{0,3,2,1:T(8,128)(2,1)}, u32[]{:S(2)}) copy-start(bf16[128,1,5,128]{0,3,2,1:T(8,128)(2,1)} %copy-done.2) | copy-start | bytes 491524
  107.8 17.5 %all-to-all-start.2 = ((f32[1,2,64,640]{3,1,0,2:T(2,128)}), f32[1,2,64,640]{3,1,0,2:T(2,128)S(1)}, u32[]{:S(2)}, u32[]{:S(2)}) async-start(f32[1,2,64,640]{3,1,0,2:T(2,128)} %reshape.235), calls=%async_computation.2 | async-start | bytes 655360 | tf_op jit(solution)/shard_map/all_to_all | solution.py:404

commit v2 on v1

--- a/solution.py
+++ b/solution.py
@@ -1,4 +1,3 @@
-import functools
 import math
 
 import jax
@@ -19,26 +18,14 @@
 ROWS = 128
 SHARD = 80
 XC, ZC = 512, 384
+N_ROLL = NX * NY * NZ
+REPEAT = HEADS // KV_HEADS
+TILE = 16
+SB = 16
+KEYS = SPAGES * PAGE
+SCALE = 1.0 / math.sqrt(HD)
+MASKED = -1e30
 MESH = pl.DeviceIdType.MESH
-
-
-MASKED = -1e30
-
-
-def softmax_parts(scores):
-    row_max = jnp.max(scores, axis=-1)
-    exponent = jnp.exp(scores - row_max[..., None])
-    row_sum = jnp.sum(exponent, axis=-1)
-    return (exponent, row_max, row_sum)
-
-
-def merge_parts(first_out, first_lse, second_out, second_lse):
-    combined = jnp.logaddexp(first_lse, second_lse)
-    mixed = (
-        jnp.exp(first_lse - combined)[..., None] * first_out
-        + jnp.exp(second_lse - combined)[..., None] * second_out
-    )
-    return mixed.astype(jnp.bfloat16)
 
 
 class Place:
@@ -97,23 +84,44 @@
 CHUNKS = ((0, 256), (256, 256), (512, 256), (768, 128))
 
 
-def project_kernel(
-    hp, w, out,
+def onehot(hit):
+    return jnp.where(hit, 1.0, 0.0).astype(jnp.bfloat16)
+
+
+def iota(shape, axis):
+    return lax.broadcasted_iota(jnp.int32, shape, axis)
+
+
+def attend_kernel(
+    hp, w, group, blocks, prefix, table, pool, out,
     wx, wz, ab, nb, ssq_s, ssq_r, cs, cr,
+    un, pref, pages, pick_send, pick_in, pick_out, pick_home,
+    q_send, q_recv, o_send, o_recv, local_out, local_lse, gathered,
     s_ss, r_ss, s_a, r_a, s_b, r_b, s_c, r_c,
     s_xz, r_xz, s_zx, r_zx, s_xx, r_xx, s_zz, r_zz,
+    load_sem, s_q, r_q, s_o, r_o,
 ):
     me = Place()
     send = Sends()
     x, y, z, t = me.x, me.y, me.z, me.t
     barrier = pltpu.get_barrier_semaphore()
     peers = [
-        me.at_z(1), me.at_z(-1), me.at_x(1), me.at_x(-1),
-        me.other(True, t), me.other(False, me.t2), me.other(True, me.t2),
+        me.other(False, me.t2), me.other(True, me.t2),
         me.other(False, me.t1), me.other(False, me.t3),
     ]
     for peer in peers:
         pl.semaphore_signal(barrier, inc=1, device_id=peer, device_id_type=MESH)
+
+    def greet(i, carry):
+        peer = {"roll": lax.rem(me.r + i, N_ROLL), "tp": t}
+        pl.semaphore_signal(barrier, inc=1, device_id=peer, device_id_type=MESH)
+        return carry
+
+    lax.fori_loop(1, N_ROLL, greet, 0)
+    load_prefix = pltpu.make_async_copy(prefix, pref, load_sem.at[0])
+    load_pages = pltpu.make_async_copy(pool, pages, load_sem.at[1])
+    load_prefix.start()
+    load_pages.start()
 
     wx[z, x] = w[:, :XC]
     wz[z, x] = w[:, XC:]
@@ -123,7 +131,7 @@
         total += jnp.sum(part * part, axis=-1, keepdims=True)
     flat = jnp.broadcast_to(total, (ROWS, ROWS)).T[:8]
     ssq_s[...] = flat
-    pl.semaphore_wait(barrier, len(peers))
+    pl.semaphore_wait(barrier, len(peers) + N_ROLL - 1)
 
     for k, tp in ((1, me.t1), (2, me.t2), (3, me.t3)):
         send(ssq_s, ssq_r.at[k], s_ss.at[k], r_ss.at[k], me.other(False, tp))
@@ -238,6 +246,44 @@
             xx_wait(d, 1, way)
             xx_send(d, 2, way)
 
+    slot = lax.shift_right_logical(group[...], 1) * TILE + jnp.bitwise_and(group[...], 1) * REPEAT
+    slot_rows = jnp.broadcast_to(slot, (ROWS, ROWS)).T
+    group_rows = jnp.broadcast_to(group[...], (ROWS, ROWS)).T
+
+    def build_send():
+        for h in range(REPEAT):
+            pick_send[:, h * ROWS : (h + 1) * ROWS] = onehot(iota((N_ROLL * TILE, ROWS), 0) == slot + h)
+
+    def build_in():
+        for i in range(2 * REPEAT):
+            target = iota((N_ROLL, N_ROLL * TILE), 0) * TILE + i
+            pick_in[i * N_ROLL : (i + 1) * N_ROLL, :] = onehot(iota((N_ROLL, N_ROLL * TILE), 1) == target)
+
+    def build_out():
+        for i in range(2 * REPEAT):
+            lane = iota((N_ROLL * TILE, ROWS), 1) + (i % REPEAT) * ROWS
+            row = lax.shift_right_logical(lane, 6) if i < REPEAT else 2 * REPEAT
+            target = jnp.bitwise_and(lane, N_ROLL - 1) * TILE + row
+            pick_out[:, i * ROWS : (i + 1) * ROWS] = onehot(iota((N_ROLL * TILE, ROWS), 0) == target)
+
+    def build_home():
+        for b in range(N_ROLL * TILE // ROWS):
+            column = iota((ROWS, ROWS), 1) + b * ROWS
+            for h in range(REPEAT):
+                pick_home[h * ROWS : (h + 1) * ROWS, b * ROWS : (b + 1) * ROWS] = onehot(column == slot_rows + h)
+            target = lax.shift_right_logical(group_rows, 1) * TILE + 2 * REPEAT
+            pick_home[REPEAT * ROWS :, b * ROWS : (b + 1) * ROWS] = onehot(column == target)
+
+    def gather_pages():
+        load_pages.wait()
+
+        def one(s, carry):
+            for j in range(SPAGES):
+                gathered[s, j] = pages[table[s, j]]
+            return carry
+
+        lax.fori_loop(0, ROWS, one, 0, unroll=8)
+
     x_first()
     xz_round(1)
     for way in both:
@@ -250,26 +296,31 @@
     for i, (tp, yy) in enumerate(((t, me.ty), (me.t2, y), (me.t2, me.ty))):
         arrived(ab.at[tp, yy], r_a.at[i])
         send(ab.at[tp, yy], ab.at[tp, yy], s_b.at[i], r_b.at[i], sibling)
+    build_send()
     xz_round(3)
     zz_round(3, 1)
     zz_round(1, 1)
     xx_round(7)
     xx_round(1)
+    build_in()
     xz_round(4)
     zz_round(2, 1)
     zz_round(0, 2)
     xx_round(6)
     xx_round(2)
+    build_out()
     zz_round(3, 2)
     zz_round(1, 2)
     zz_round(2, 2)
     xx_round(5)
     xx_round(3)
+    build_home()
     zz_round(0, 3)
     zz_round(3, 3)
     zz_round(1, 3)
     zz_round(2, 3)
     xx_round(4)
+    gather_pages()
     for i, (tp, yy) in enumerate(
         ((me.t1, me.ty), (me.t3, y), (me.t3, me.ty), (me.t1, y))
     ):
@@ -297,131 +348,159 @@
         )
     for i, (start, width) in enumerate(CHUNKS):
         arrived(cr.at[i, :, pl.ds(0, width)], r_c.at[i])
-        out[:, start : start + width] = (cs[i, y, :, :width] + cr[i, :, :width]).astype(jnp.bfloat16)
+        un[:, start : start + width] = (cs[i, y, :, :width] + cr[i, :, :width]).astype(jnp.bfloat16)
+
+    rows = jnp.concatenate([un[:, h * HD : (h + 1) * HD] for h in range(REPEAT)], axis=0)
+    q_send[...] = jnp.dot(pick_send[...], rows, preferred_element_type=jnp.float32).astype(
+        jnp.bfloat16
+    ).reshape(N_ROLL, TILE, HD)
+
+    def exchange(src, dst, s_sem, r_sem):
+        def one(i, carry):
+            peer = lax.rem(me.r + i, N_ROLL)
+            pltpu.make_async_remote_copy(
+                src_ref=src.at[peer], dst_ref=dst.at[me.r], send_sem=s_sem, recv_sem=r_sem,
+                device_id={"roll": peer, "tp": t}, device_id_type=MESH,
+            ).start()
+            return carry
+
+        lax.fori_loop(1, N_ROLL, one, 0)
+        dst[me.r] = src[me.r]
+
+    exchange(q_send, q_recv, s_q, r_q)
+
+    def local_block(b, carry):
+        at = pl.ds(pl.multiple_of(b * SB, SB), SB)
+        queries = jnp.concatenate([un[at, h * HD : (h + 1) * HD] for h in range(REPEAT)], axis=0)
+        own_k = un[at, REPEAT * HD : (REPEAT + 1) * HD].astype(jnp.float32)
+        own_v = un[at, (REPEAT + 1) * HD :].astype(jnp.float32)
+        own_k = jnp.concatenate([own_k] * REPEAT, axis=0)
+        own_v = jnp.concatenate([own_v] * REPEAT, axis=0)
+        keys = gathered[at, :, :, :HD].reshape(SB * KEYS, HD)
+        values = gathered[at, :, :, HD:].reshape(SB * KEYS, HD)
+        scores = lax.dot_general(
+            queries, keys, (((1,), (1,)), ((), ())), preferred_element_type=jnp.float32
+        ) * SCALE
+        shape = (REPEAT * SB, SB * KEYS)
+        mine = jnp.bitwise_and(iota(shape, 0), SB - 1) == lax.shift_right_logical(iota(shape, 1), 5)
+        scores = jnp.where(mine, scores, MASKED)
+        own = jnp.sum(queries.astype(jnp.float32) * own_k, axis=-1, keepdims=True) * SCALE
+        top = jnp.maximum(jnp.max(scores, axis=-1, keepdims=True), own)
+        e = jnp.exp(scores - top)
+        e_own = jnp.exp(own - top)
+        total = jnp.sum(e, axis=-1, keepdims=True) + e_own
+        weights = (e / total).astype(jnp.bfloat16)
+        w_own = (e_own / total).astype(jnp.bfloat16).astype(jnp.float32)
+        res = jnp.dot(weights, values, preferred_element_type=jnp.float32) + w_own * own_v
+        lse = jnp.broadcast_to(top + jnp.log(total), (REPEAT * SB, HD))
+        for h in range(REPEAT):
+            local_out[h, at, :] = res[h * SB : (h + 1) * SB]
+            local_lse[h, at, :] = lse[h * SB : (h + 1) * SB]
+        return carry
+
+    lax.fori_loop(0, ROWS // SB, local_block, 0)
+
+    load_prefix.wait()
+    arrived(q_recv.at[pl.ds(0, N_ROLL - 1)], r_q)
+    came = q_recv[...].reshape(N_ROLL * TILE, HD)
+    outs, marks = [], []
+    per = REPEAT * N_ROLL
+    for j in range(2):
+        queries = jnp.dot(
+            pick_in[j * per : (j + 1) * per, :], came, preferred_element_type=jnp.float32
+        ).astype(jnp.bfloat16)
+        scores = lax.dot_general(
+            queries, pref[j, :, :HD], (((1,), (1,)), ((), ())), preferred_element_type=jnp.float32
+        ) * SCALE
+        scores = jnp.where(iota(scores.shape, 1) < blocks[j] * BLOCK, scores, MASKED)
+        top = jnp.max(scores, axis=-1, keepdims=True)
+        e = jnp.exp(scores - top)
+        total = jnp.sum(e, axis=-1, keepdims=True)
+        weights = (e / total).astype(jnp.bfloat16)
+        res = jnp.dot(weights, pref[j, :, HD:], preferred_element_type=jnp.float32)
+        outs.append(res.astype(jnp.bfloat16))
+        lse = jnp.broadcast_to(top + jnp.log(total), (per, HD))
+        hi = lse.astype(jnp.bfloat16).astype(jnp.float32)
+        mid = (lse - hi).astype(jnp.bfloat16).astype(jnp.float32)
+        low = lse - hi - mid
+        lane = iota((per, HD), 1)
+        first = (lax.shift_right_logical(iota((per, HD), 0), 6) + j * REPEAT) * 3
+        mark = jnp.where(lane == first, hi, jnp.where(lane == first + 1, mid, jnp.where(lane == first + 2, low, 0.0)))
+        marks.append(mark.astype(jnp.bfloat16))
+    stacked = jnp.concatenate(outs + marks, axis=0)
+    o_send[...] = jnp.dot(pick_out[...], stacked, preferred_element_type=jnp.float32).astype(
+        jnp.bfloat16
+    ).reshape(N_ROLL, TILE, HD)
+    exchange(o_send, o_recv, s_o, r_o)
+
+    arrived(o_recv.at[pl.ds(0, N_ROLL - 1)], r_o)
+    back = jnp.dot(
+        pick_home[...], o_recv[...].reshape(N_ROLL * TILE, HD), preferred_element_type=jnp.float32
+    )
+    terms = back[REPEAT * ROWS :]
+    second = jnp.bitwise_and(group_rows, 1) * REPEAT
+    lane = iota((ROWS, HD), 1)
+    for h in range(REPEAT):
+        first = (second + h) * 3
+        mine = jnp.where((lane >= first) & (lane < first + 3), terms, 0.0)
+        p_lse = jnp.broadcast_to(jnp.sum(mine, axis=-1, keepdims=True), (ROWS, HD))
+        l_lse = local_lse[h]
+        top = jnp.maximum(p_lse, l_lse)
+        ep = jnp.exp(p_lse - top)
+        el = jnp.exp(l_lse - top)
+        mixed = (ep * back[h * ROWS : (h + 1) * ROWS] + el * local_out[h]) / (ep + el)
+        out[:, h * HD : (h + 1) * HD] = mixed.astype(jnp.bfloat16)
+
+    arrived(q_send.at[pl.ds(0, N_ROLL - 1)], s_q)
+    arrived(o_send.at[pl.ds(0, N_ROLL - 1)], s_o)
     send.finish()
 
 
-def project(hidden_in, qkv_weight):
+def per_device(
+    hidden_in, qkv_weight, sample_group, prefix_blocks, prefix_kv, page_table, suffix_pool
+):
     hp = hidden_in.reshape(ROWS, 2, 2, 320).transpose(2, 0, 1, 3).reshape(2, ROWS, 640)
     dma = pltpu.SemaphoreType.DMA
     vmem = pl.BlockSpec(memory_space=pltpu.VMEM)
+    smem = pl.BlockSpec(memory_space=pltpu.SMEM)
+    hbm = pl.BlockSpec(memory_space=pl.ANY)
+    bf16, f32 = jnp.bfloat16, jnp.float32
     sems = []
     for shape in ((4,), (3,), (4,), (4,), (8,), (4,), (8, 4), (4, 8)):
         sems += [dma(shape), dma(shape)]
+    tiles = pltpu.VMEM((N_ROLL, TILE, HD), bf16)
     return pl.pallas_call(
-        project_kernel,
-        out_shape=jax.ShapeDtypeStruct((ROWS, XC + ZC), jnp.bfloat16),
-        in_specs=[vmem, vmem],
+        attend_kernel,
+        out_shape=jax.ShapeDtypeStruct((ROWS, REPEAT * HD), bf16),
+        in_specs=[vmem, vmem, vmem, smem, hbm, smem, hbm],
         out_specs=vmem,
         scratch_shapes=[
-            pltpu.VMEM((NZ, NX, SHARD, XC), jnp.bfloat16),
-            pltpu.VMEM((NZ, NX, SHARD, ZC), jnp.bfloat16),
-            pltpu.VMEM((4, 2, ROWS, 640), jnp.bfloat16),
-            pltpu.VMEM((2, ROWS, 640), jnp.bfloat16),
-            pltpu.VMEM((8, ROWS), jnp.float32),
-            pltpu.VMEM((4, 8, ROWS), jnp.float32),
-            pltpu.VMEM((4, 2, ROWS, 256), jnp.float32),
-            pltpu.VMEM((4, ROWS, 256), jnp.float32),
+            pltpu.VMEM((NZ, NX, SHARD, XC), bf16),
+            pltpu.VMEM((NZ, NX, SHARD, ZC), bf16),
+            pltpu.VMEM((4, 2, ROWS, 640), bf16),
+            pltpu.VMEM((2, ROWS, 640), bf16),
+            pltpu.VMEM((8, ROWS), f32),
+            pltpu.VMEM((4, 8, ROWS), f32),
+            pltpu.VMEM((4, 2, ROWS, 256), f32),
+            pltpu.VMEM((4, ROWS, 256), f32),
+            pltpu.VMEM((ROWS, XC + ZC), bf16),
+            pltpu.VMEM(prefix_kv.shape, bf16),
+            pltpu.VMEM(suffix_pool.shape, bf16),
+            pltpu.VMEM((N_ROLL * TILE, REPEAT * ROWS), bf16),
+            pltpu.VMEM((2 * REPEAT * N_ROLL, N_ROLL * TILE), bf16),
+            pltpu.VMEM((N_ROLL * TILE, 2 * REPEAT * ROWS), bf16),
+            pltpu.VMEM(((REPEAT + 1) * ROWS, N_ROLL * TILE), bf16),
+            tiles, tiles, tiles, tiles,
+            pltpu.VMEM((REPEAT, ROWS, HD), f32),
+            pltpu.VMEM((REPEAT, ROWS, HD), f32),
+            pltpu.VMEM((ROWS, SPAGES, PAGE, 2 * HD), bf16),
             *sems,
+            dma((2,)), dma, dma, dma, dma,
         ],
         compiler_params=pltpu.CompilerParams(
-            collective_id=0, has_side_effects=True, vmem_limit_bytes=40 * 1024 * 1024
+            collective_id=0, has_side_effects=True, vmem_limit_bytes=48 * 1024 * 1024
         ),
-    )(hp, qkv_weight)
-
-
-def per_device(
-    hidden_in, qkv_weight, sample_group, prefix_blocks, prefix_kv, page_table, suffix_pool
-):
-    row_count = hidden_in.shape[0]
-    kv_heads_dev = prefix_kv.shape[2] // (2 * HD)
-    repeat = HEADS // KV_HEADS
-    q_width = kv_heads_dev * repeat * HD
-    head_count = kv_heads_dev * repeat
-    owned_groups = prefix_kv.shape[0]
-    roll_count = lax.axis_size("roll")
-    per_group = row_count // (roll_count * owned_groups)
-    owner_rows = roll_count * per_group
-    prefix_span = prefix_kv.shape[1]
-    score_scale = 1.0 / math.sqrt(HD)
-    united_proj = project(hidden_in, qkv_weight)
-    united_proj = united_proj.astype(jnp.bfloat16).reshape(row_count, kv_heads_dev, repeat + 2, HD)
-    queries = united_proj[:, :, :repeat]
-    own_key = united_proj[:, :, repeat]
-    own_value = united_proj[:, :, repeat + 1]
-    sort_order = jnp.argsort(sample_group, stable=True)
-
-    def sample_layout(arrived, width, dtype):
-        return (
-            jnp.zeros((row_count, width), dtype)
-            .at[sort_order]
-            .set(arrived.reshape(row_count, width))
-        )
-
-    page_rows = suffix_pool[page_table].reshape(row_count, SPAGES * PAGE, kv_heads_dev, 2, HD)
-    key_rows = jnp.concatenate([page_rows[:, :, :, 0], own_key[:, None]], axis=1)
-    value_rows = jnp.concatenate([page_rows[:, :, :, 1], own_value[:, None]], axis=1)
-    scores = (
-        jnp.einsum("sjrd,stjd->sjrt", queries, key_rows, preferred_element_type=jnp.float32)
-        * score_scale
-    )
-    exponent, row_max, row_sum = softmax_parts(scores)
-    weights = (exponent / row_sum[..., None]).astype(jnp.bfloat16)
-    result = jnp.einsum("sjrt,stjd->sjrd", weights, value_rows, preferred_element_type=jnp.float32)
-    local_out = result
-    local_lse = row_max + jnp.log(row_sum)
-    incoming = lax.all_to_all(
-        queries.reshape(row_count, q_width)[sort_order].reshape(
-            roll_count, owned_groups, per_group, q_width
-        ),
-        "roll",
-        split_axis=0,
-        concat_axis=2,
-        tiled=True,
-    )
-    kv_cache = prefix_kv.reshape(owned_groups, prefix_span, kv_heads_dev, 2, HD)
-    scores = (
-        jnp.einsum(
-            "gqjrd,gtjd->gqjrt",
-            incoming.reshape(owned_groups, owner_rows, kv_heads_dev, repeat, HD),
-            kv_cache[:, :, :, 0],
-            preferred_element_type=jnp.float32,
-        )
-        * score_scale
-    )
-    live_mask = (jnp.arange(prefix_span)[None, :] < prefix_blocks[:, None] * BLOCK)[
-        :, None, None, None, :
-    ]
-    scores = jnp.where(live_mask, scores, MASKED)
-    row_max = jnp.max(scores, axis=-1)
-    exponent = jnp.where(live_mask, jnp.exp(scores - row_max[..., None]), 0.0)
-    row_sum = jnp.sum(exponent, axis=-1)
-    weights = (exponent / row_sum[..., None]).astype(jnp.bfloat16)
-    result = jnp.einsum(
-        "gqjrt,gtjd->gqjrd", weights, kv_cache[:, :, :, 1], preferred_element_type=jnp.float32
-    )
-    result, result_lse = (result, row_max + jnp.log(row_sum))
-    back_out = lax.all_to_all(
-        result.reshape(1, owned_groups, owner_rows, q_width),
-        "roll",
-        split_axis=2,
-        concat_axis=0,
-        tiled=True,
-    )
-    back_lse = lax.all_to_all(
-        result_lse.reshape(1, owned_groups, owner_rows, head_count),
-        "roll",
-        split_axis=2,
-        concat_axis=0,
-        tiled=True,
-    )
-    prefix_out = sample_layout(back_out, q_width, jnp.float32)
-    prefix_lse = sample_layout(back_lse, head_count, jnp.float32)
-    prefix_out, prefix_lse = (
-        prefix_out.reshape(row_count, kv_heads_dev, repeat, HD),
-        prefix_lse.reshape(row_count, kv_heads_dev, repeat),
-    )
-    return merge_parts(prefix_out, prefix_lse, local_out, local_lse).reshape(row_count, q_width)
+    )(hp, qkv_weight, sample_group.reshape(1, ROWS), prefix_blocks, prefix_kv, page_table, suffix_pool)
 
 
 def solution(mesh):

time: 131 us -> 82.6 us (0.63)
  local copies, waits for them, and re-layouts: 32.5 us -> 5.84 us
  Pallas kernels: 50.5 us -> 76.4 us
  starting transfers between devices: 24.3 us -> 0 us
  waiting for transfers between devices: 12.7 us -> 0 us
  matrix products: 7.06 us -> 0 us
  other arithmetic: 3.49 us -> 0 us
    pallas_call x1, Pallas kernels: 50.5 us -> 76.4 us  [per_device(): pl.pallas_call(attend_kernel, out_shape=jax.ShapeDtypeStruct((ROWS, REPEA...]
    all_to_all x3 -> x0, starting transfers between devices: 24.3 us -> none  [the longest x1 11.2 us: per_device(): lax.all_to_all(result_lse.reshape(1, owned_groups, owner_rows, head_count...]
    all_to_all x3 -> x0, waiting for transfers between devices: 12.7 us -> none  [the longest x1 7.19 us: per_device(): lax.all_to_all(result_lse.reshape(1, owned_groups, owner_rows, head_count...]
    slice x3 -> x0, local copies, waits for them, and re-layouts: 8.27 us -> none  [the longest x1 7.48 us: per_device(): page_rows[:, :, :, 0]]
    reshape x9 -> x1, local copies, waits for them, and re-layouts: 8.24 us -> 0.21 us  [per_device(): hidden_in.reshape(ROWS, 2, 2, 320).transpose(2, 0, 1, 3)]
    dot_general x4 -> x0, matrix products: 7.06 us -> none  [the longest x1 2.18 us: per_device(): jnp.einsum('sjrd,stjd->sjrt', queries, key_rows, preferred_element_type=j...]
    squeeze x1 -> x0, local copies, waits for them, and re-layouts: 4.05 us -> none  [per_device(): page_rows[:, :, :, 1]]
    gather x2 -> x0, local copies, waits for them, and re-layouts: 2.99 us -> none  [the longest x1 2.11 us: per_device(): suffix_pool[page_table]]
  transfers between devices with their start and end apart: 3 -> 0, of which waited for: 2 -> 0; matrix products, arithmetic and copies ran while one was open for 21% -> 0% of each run, Pallas kernels for 0% -> 0%
where the time goes in v2:
time: 82.6 us; the launch traced here: 82.3 us
  Pallas kernels  76.4 us (92%)
  local copies, waits for them, and re-layouts  5.84 us (7%)
    pallas_call x1, Pallas kernels, per_device(): pl.pallas_call(attend_kernel, out_shape=jax.ShapeDtypeStruct((ROWS, REPEA...  76.4 us
    unnamed x13, local copies, waits for them, and re-layouts  5.6 us

profile of v2, /device:TPU:8, one launch (start us, length us, event | category | flops | bytes accessed | tf_op | source)
XLA Modules:
  0.0 82.3 jit_solution(15199900854491783979)
XLA Ops:
  0.0 0.0 copy-start.1
  0.0 0.0 copy-start.2
  0.0 1.2 %copy.10 = bf16[128,1280]{0,1:T(8,128)(2,1)S(1)} copy(bf16[128,1280]{1,0:T(8,128)(2,1)} %param.7) | data formatting | bytes 655360 | tf_op args[0]
  1.3 0.2 copy.12.hp
  1.5 0.8 copy.13.table
  2.3 0.0 copy-done.1
  2.3 0.0 copy-done.2
  2.3 0.0 copy-start
  2.3 1.6 %copy-done = bf16[256,16,256]{2,1,0:T(8,128)(2,1)S(1)} copy-done((bf16[256,16,256]{2,1,0:T(8,128)(2,1)S(1)}, bf16[256,16,256]{2,1,0:T(8,128)(2,1)}, u32[]{:S(2)}) %copy-start) | copy-done | bytes 2097176
  3.9 0.0 copy-start.3
  3.9 0.7 copy-done.3
  4.6 0.0 copy-start.4
  4.6 0.7 copy-done.4
  5.2 76.4 %shard_map.73 = bf16[128,640]{1,0:T(8,128)(2,1)S(1)} custom-call(bf16[2,128,640]{2,1,0:T(8,128)(2,1)S(1)} %copy.12.hp, bf16[80,896]{1,0:T(8,128)(2,1)S(1)} %copy-done.2, s32[1,128]{1,0:T(1,128)S(1)} %bitcast.5, s32[2]{0:T(128)S(1)} %copy-done.4, bf16[2,512,256]{2,1,0:T(8,128)(2,1)S(1)} %copy-done.1, s32[128,2]{1,0:T(8,128)S(1)} %copy.13.table, ...), custom_call_target="tpu_custom_call" | custom-call | tf_op jit(solution)/shard_map/pallas_call | solution.py:472
  81.6 0.7 copy.15
  (1 shorter events, 0.0 us)
Async XLA Ops:
  0.0 2.3 %copy-start.1 = (bf16[2,512,256]{2,1,0:T(8,128)(2,1)S(1)}, bf16[2,512,256]{2,1,0:T(8,128)(2,1)}, u32[]{:S(2)}) copy-start(bf16[2,512,256]{2,1,0:T(8,128)(2,1)} %prefix.1) | copy-start | bytes 1572868
  0.0 2.3 %copy-start.2 = (bf16[80,896]{1,0:T(8,128)(2,1)S(1)}, bf16[80,896]{1,0:T(8,128)(2,1)}, u32[]{:S(2)}) copy-start(bf16[80,896]{1,0:T(8,128)(2,1)} %w.1) | copy-start | bytes 430084
  2.3 1.6 %copy-start = (bf16[256,16,256]{2,1,0:T(8,128)(2,1)S(1)}, bf16[256,16,256]{2,1,0:T(8,128)(2,1)}, u32[]{:S(2)}) copy-start(bf16[256,16,256]{2,1,0:T(8,128)(2,1)} %pool.1) | copy-start | bytes 6291460
  3.9 0.7 copy-start.3
  4.6 0.7 copy-start.4

commit v3 on v2

--- a/solution.py
+++ b/solution.py
@@ -93,7 +93,8 @@
 
 
 def attend_kernel(
-    hp, w, group, blocks, prefix, table, pool, out,
+    hidden_hbm, w_hbm, group_hbm, blocks, prefix, table_hbm, pool, out,
+    hidden, w, group, table,
     wx, wz, ab, nb, ssq_s, ssq_r, cs, cr,
     un, pref, pages, pick_send, pick_in, pick_out, pick_home,
     q_send, q_recv, o_send, o_recv, local_out, local_lse, gathered,
@@ -106,32 +107,77 @@
     x, y, z, t = me.x, me.y, me.z, me.t
     barrier = pltpu.get_barrier_semaphore()
     peers = [
-        me.other(False, me.t2), me.other(True, me.t2),
+        me.at_z(1), me.at_z(-1), me.at_x(1), me.at_x(-1),
+        me.other(True, t), me.other(False, me.t2), me.other(True, me.t2),
         me.other(False, me.t1), me.other(False, me.t3),
     ]
     for peer in peers:
         pl.semaphore_signal(barrier, inc=1, device_id=peer, device_id_type=MESH)
-
-    def greet(i, carry):
-        peer = {"roll": lax.rem(me.r + i, N_ROLL), "tp": t}
-        pl.semaphore_signal(barrier, inc=1, device_id=peer, device_id_type=MESH)
-        return carry
-
-    lax.fori_loop(1, N_ROLL, greet, 0)
+    load_hidden = pltpu.make_async_copy(hidden_hbm, hidden, load_sem.at[2])
+    load_w = pltpu.make_async_copy(w_hbm, w, load_sem.at[3])
+    load_group = pltpu.make_async_copy(group_hbm, group, load_sem.at[4])
+    load_table = pltpu.make_async_copy(table_hbm, table, load_sem.at[5])
+    load_hidden.start()
+    load_w.start()
+    load_group.start()
+    load_table.start()
     load_prefix = pltpu.make_async_copy(prefix, pref, load_sem.at[0])
     load_pages = pltpu.make_async_copy(pool, pages, load_sem.at[1])
     load_prefix.start()
     load_pages.start()
 
+    load_w.wait()
     wx[z, x] = w[:, :XC]
     wz[z, x] = w[:, XC:]
-    total = jnp.zeros((ROWS, 1), jnp.float32)
-    for side in range(2):
-        part = hp[side].astype(jnp.float32)
-        total += jnp.sum(part * part, axis=-1, keepdims=True)
+    load_hidden.wait()
+    total = jnp.zeros((ROWS, HD), jnp.float32)
+    for b in range(10):
+        part = hidden[:, b * HD : (b + 1) * HD].astype(jnp.float32)
+        total += part * part
+    total = jnp.sum(total, axis=-1, keepdims=True)
     flat = jnp.broadcast_to(total, (ROWS, ROWS)).T[:8]
     ssq_s[...] = flat
-    pl.semaphore_wait(barrier, len(peers) + N_ROLL - 1)
+    load_group.wait()
+    load_table.wait()
+    slot = lax.shift_right_logical(group[...], 1) * TILE + jnp.bitwise_and(group[...], 1) * REPEAT
+    slot_rows = jnp.broadcast_to(slot, (ROWS, ROWS)).T
+    group_rows = jnp.broadcast_to(group[...], (ROWS, ROWS)).T
+
+    def build_send():
+        for h in range(REPEAT):
+            pick_send[:, h * ROWS : (h + 1) * ROWS] = onehot(iota((N_ROLL * TILE, ROWS), 0) == slot + h)
+
+    def build_in():
+        for i in range(2 * REPEAT):
+            target = iota((N_ROLL, N_ROLL * TILE), 0) * TILE + i
+            pick_in[i * N_ROLL : (i + 1) * N_ROLL, :] = onehot(iota((N_ROLL, N_ROLL * TILE), 1) == target)
+
+    def build_out():
+        for i in range(2 * REPEAT):
+            lane = iota((N_ROLL * TILE, ROWS), 1) + (i % REPEAT) * ROWS
+            row = lax.shift_right_logical(lane, 6) if i < REPEAT else 2 * REPEAT
+            target = jnp.bitwise_and(lane, N_ROLL - 1) * TILE + row
+            pick_out[:, i * ROWS : (i + 1) * ROWS] = onehot(iota((N_ROLL * TILE, ROWS), 0) == target)
+
+    def build_home():
+        for b in range(N_ROLL * TILE // ROWS):
+            column = iota((ROWS, ROWS), 1) + b * ROWS
+            for h in range(REPEAT):
+                pick_home[h * ROWS : (h + 1) * ROWS, b * ROWS : (b + 1) * ROWS] = onehot(column == slot_rows + h)
+            target = lax.shift_right_logical(group_rows, 1) * TILE + 2 * REPEAT
+            pick_home[REPEAT * ROWS :, b * ROWS : (b + 1) * ROWS] = onehot(column == target)
+
+    def gather_pages():
+        load_pages.wait()
+
+        def one(s, carry):
+            for j in range(SPAGES):
+                gathered[s, j] = pages[table[j, s]]
+            return carry
+
+        lax.fori_loop(0, ROWS, one, 0, unroll=8)
+
+    pl.semaphore_wait(barrier, len(peers))
 
     for k, tp in ((1, me.t1), (2, me.t2), (3, me.t3)):
         send(ssq_s, ssq_r.at[k], s_ss.at[k], r_ss.at[k], me.other(False, tp))
@@ -203,10 +249,20 @@
         ssum += ssq_r[k]
     scale = lax.rsqrt(ssum / D + 1e-06)
     scale = jnp.broadcast_to(scale[:1], (ROWS, ROWS)).T
+    tiles = [hidden[:, b * HD : (b + 1) * HD].astype(jnp.float32) * scale for b in range(10)]
+    turned = {b: pltpu.roll(tiles[b], HD // 2, 1) for b in range(2, 8)}
+    low_half = iota((ROWS, HD), 1) < HD // 2
+
+    def halves(first, second):
+        return jnp.where(low_half, first, second)
+
+    sides = (
+        (tiles[0], tiles[1], halves(tiles[2], turned[5]), halves(turned[5], turned[6]), halves(turned[6], turned[7])),
+        (halves(turned[2], turned[3]), halves(turned[3], turned[4]), halves(turned[4], tiles[7]), tiles[8], tiles[9]),
+    )
     for side in range(2):
         for b in range(5):
-            cols = slice(b * 128, b * 128 + 128)
-            nb[side, :, cols] = (hp[side, :, cols].astype(jnp.float32) * scale).astype(jnp.bfloat16)
+            nb[side, :, b * HD : (b + 1) * HD] = sides[side][b].astype(jnp.bfloat16)
     ab[t, y] = nb[y]
     send(nb.at[me.ty], ab.at[t, y], s_a.at[0], r_a.at[0], me.other(True, t))
     send(nb.at[y], ab.at[t, y], s_a.at[1], r_a.at[1], me.other(False, me.t2))
@@ -246,46 +302,10 @@
             xx_wait(d, 1, way)
             xx_send(d, 2, way)
 
-    slot = lax.shift_right_logical(group[...], 1) * TILE + jnp.bitwise_and(group[...], 1) * REPEAT
-    slot_rows = jnp.broadcast_to(slot, (ROWS, ROWS)).T
-    group_rows = jnp.broadcast_to(group[...], (ROWS, ROWS)).T
-
-    def build_send():
-        for h in range(REPEAT):
-            pick_send[:, h * ROWS : (h + 1) * ROWS] = onehot(iota((N_ROLL * TILE, ROWS), 0) == slot + h)
-
-    def build_in():
-        for i in range(2 * REPEAT):
-            target = iota((N_ROLL, N_ROLL * TILE), 0) * TILE + i
-            pick_in[i * N_ROLL : (i + 1) * N_ROLL, :] = onehot(iota((N_ROLL, N_ROLL * TILE), 1) == target)
-
-    def build_out():
-        for i in range(2 * REPEAT):
-            lane = iota((N_ROLL * TILE, ROWS), 1) + (i % REPEAT) * ROWS
-            row = lax.shift_right_logical(lane, 6) if i < REPEAT else 2 * REPEAT
-            target = jnp.bitwise_and(lane, N_ROLL - 1) * TILE + row
-            pick_out[:, i * ROWS : (i + 1) * ROWS] = onehot(iota((N_ROLL * TILE, ROWS), 0) == target)
-
-    def build_home():
-        for b in range(N_ROLL * TILE // ROWS):
-            column = iota((ROWS, ROWS), 1) + b * ROWS
-            for h in range(REPEAT):
-                pick_home[h * ROWS : (h + 1) * ROWS, b * ROWS : (b + 1) * ROWS] = onehot(column == slot_rows + h)
-            target = lax.shift_right_logical(group_rows, 1) * TILE + 2 * REPEAT
-            pick_home[REPEAT * ROWS :, b * ROWS : (b + 1) * ROWS] = onehot(column == target)
-
-    def gather_pages():
-        load_pages.wait()
-
-        def one(s, carry):
-            for j in range(SPAGES):
-                gathered[s, j] = pages[table[s, j]]
-            return carry
-
-        lax.fori_loop(0, ROWS, one, 0, unroll=8)
-
+    build_send()
     x_first()
     xz_round(1)
+    build_in()
     for way in both:
         zx_wait(2, way)
     for way in both:
@@ -296,25 +316,23 @@
     for i, (tp, yy) in enumerate(((t, me.ty), (me.t2, y), (me.t2, me.ty))):
         arrived(ab.at[tp, yy], r_a.at[i])
         send(ab.at[tp, yy], ab.at[tp, yy], s_b.at[i], r_b.at[i], sibling)
-    build_send()
+    build_out()
     xz_round(3)
     zz_round(3, 1)
     zz_round(1, 1)
     xx_round(7)
     xx_round(1)
-    build_in()
     xz_round(4)
     zz_round(2, 1)
     zz_round(0, 2)
     xx_round(6)
     xx_round(2)
-    build_out()
+    build_home()
     zz_round(3, 2)
     zz_round(1, 2)
     zz_round(2, 2)
     xx_round(5)
     xx_round(3)
-    build_home()
     zz_round(0, 3)
     zz_round(3, 3)
     zz_round(1, 3)
@@ -459,7 +477,6 @@
 def per_device(
     hidden_in, qkv_weight, sample_group, prefix_blocks, prefix_kv, page_table, suffix_pool
 ):
-    hp = hidden_in.reshape(ROWS, 2, 2, 320).transpose(2, 0, 1, 3).reshape(2, ROWS, 640)
     dma = pltpu.SemaphoreType.DMA
     vmem = pl.BlockSpec(memory_space=pltpu.VMEM)
     smem = pl.BlockSpec(memory_space=pltpu.SMEM)
@@ -472,9 +489,13 @@
     return pl.pallas_call(
         attend_kernel,
         out_shape=jax.ShapeDtypeStruct((ROWS, REPEAT * HD), bf16),
-        in_specs=[vmem, vmem, vmem, smem, hbm, smem, hbm],
+        in_specs=[hbm, hbm, hbm, smem, hbm, hbm, hbm],
         out_specs=vmem,
         scratch_shapes=[
+            pltpu.VMEM((ROWS, 10 * HD), bf16),
+            pltpu.VMEM((SHARD, XC + ZC), bf16),
+            pltpu.VMEM((1, ROWS), jnp.int32),
+            pltpu.SMEM((SPAGES, ROWS), jnp.int32),
             pltpu.VMEM((NZ, NX, SHARD, XC), bf16),
             pltpu.VMEM((NZ, NX, SHARD, ZC), bf16),
             pltpu.VMEM((4, 2, ROWS, 640), bf16),
@@ -495,12 +516,12 @@
             pltpu.VMEM((REPEAT, ROWS, HD), f32),
             pltpu.VMEM((ROWS, SPAGES, PAGE, 2 * HD), bf16),
             *sems,
-            dma((2,)), dma, dma, dma, dma,
+            dma((6,)), dma, dma, dma, dma,
         ],
         compiler_params=pltpu.CompilerParams(
-            collective_id=0, has_side_effects=True, vmem_limit_bytes=48 * 1024 * 1024
+            collective_id=0, has_side_effects=True, vmem_limit_bytes=62 * 1024 * 1024
         ),
-    )(hp, qkv_weight, sample_group.reshape(1, ROWS), prefix_blocks, prefix_kv, page_table, suffix_pool)
+    )(hidden_in, qkv_weight, sample_group.reshape(1, ROWS), prefix_blocks, prefix_kv, page_table.T, suffix_pool)
 
 
 def solution(mesh):

time: 82.6 us -> 76.8 us (0.930)
  local copies, waits for them, and re-layouts: 5.84 us -> 1.6 us
  Pallas kernels: 76.4 us -> 75 us
    unnamed x13 -> x1, local copies, waits for them, and re-layouts: 5.6 us -> 1.6 us
    pallas_call x1, Pallas kernels: 76.4 us -> 75 us  [per_device(): pl.pallas_call(attend_kernel, out_shape=jax.ShapeDtypeStruct((ROWS, REPEA...]
where the time goes in v3:
time: 76.8 us; the launch traced here: 76.6 us
  Pallas kernels  75 us (98%)
  local copies, waits for them, and re-layouts  1.6 us (2%)
    pallas_call x1, Pallas kernels, per_device(): pl.pallas_call(attend_kernel, out_shape=jax.ShapeDtypeStruct((ROWS, REPEA...  75 us
    unnamed x1, local copies, waits for them, and re-layouts  1.6 us

profile of v3, /device:TPU:8, one launch (start us, length us, event | category | flops | bytes accessed | tf_op | source)
XLA Modules:
  0.0 76.6 jit_solution(15147307956897764976)
XLA Ops:
  0.0 75.0 %shard_map.73 = bf16[128,640]{1,0:T(8,128)(2,1)} custom-call(bf16[128,1280]{1,0:T(8,128)(2,1)} %hidden_hbm.1, bf16[80,896]{1,0:T(8,128)(2,1)} %w_hbm.1, s32[1,128]{1,0:T(1,128)} %bitcast.3, s32[2]{0:T(128)} %blocks.1, bf16[2,512,256]{2,1,0:T(8,128)(2,1)} %prefix.1, s32[2,128]{1,0:T(2,128)} %bitcast.2, bf16[256,16,256]{2,1,0:T(8,128)(2,1)} %pool.1), custom_call_target="tpu_custom_call" | custom-call | tf_op jit(solution)/shard_map/pallas_call | solution.py:489
  75.0 1.6 %copy.9 = bf16[128,640]{1,0:T(8,128)(2,1)} copy(bf16[128,640]{1,0:T(8,128)(2,1)} %shard_map.73) | data formatting | bytes 327680

commit v4 on v3

--- a/solution.py
+++ b/solution.py
@@ -17,7 +17,7 @@
 NX, NY, NZ = 4, 2, 8
 ROWS = 128
 SHARD = 80
-XC, ZC = 512, 384
+QX, QZ, KX, VZ = 384, 256, 128, 128
 N_ROLL = NX * NY * NZ
 REPEAT = HEADS // KV_HEADS
 TILE = 16
@@ -26,6 +26,31 @@
 SCALE = 1.0 / math.sqrt(HD)
 MASKED = -1e30
 MESH = pl.DeviceIdType.MESH
+ORDER = (
+    (
+        514, 515, 2, 3, 770, 771, 258, 259, 516, 517, 818, 819,
+    ),
+    (
+        370, 786, 787, 371, 274, 4, 5, 275, 260, 261, 772, 773, 372, 802, 803, 373, 820, 821,
+        276,
+    ),
+    (
+        788, 789, 355, 354, 6, 7, 291, 290, 774, 775, 277, 357, 804, 805, 356, 822,
+    ),
+    (
+        823, 790, 791, 338, 339, 1027, 1282, 1283, 8, 1795, 1538, 1539, 1026, 9, 1794, 777, 776, 306,
+        307, 807, 293, 806, 292, 825, 824, 340, 341, 793, 792, 1298, 1299, 1029, 1842, 1285, 1284, 1797,
+        1810, 1843, 1028, 1811, 1796, 323, 322, 809, 1540, 1541, 808, 1394, 1395, 308, 1300, 1031, 309, 1844,
+        1301, 1314, 1799, 1812, 1315, 1378, 1845, 1030, 1379, 1813, 1798, 325, 324,
+    ),
+    (
+        1827, 1826, 1396, 1397, 1033, 1330, 1331, 1801, 1846, 1316, 1317, 1814, 1380, 1847, 1032, 1363, 1362, 1381,
+        1800, 1815, 1829, 1828, 1332,
+    ),
+    (
+        1333, 1848, 1816, 1849, 1346, 1347, 1364, 1817, 1365, 1831, 1830, 1349, 1348, 1833, 1832,
+    ),
+)
 
 
 class Place:
@@ -81,7 +106,86 @@
     pltpu.make_async_copy(ref, ref, sem).wait()
 
 
-CHUNKS = ((0, 256), (256, 256), (512, 256), (768, 128))
+class Gather:
+    def __init__(self, me, send, wx, wz, sems):
+        self.me, self.send, self.wx, self.wz = me, send, wx, wz
+        self.seen = set()
+        self.s_xz, self.r_xz, self.s_zx, self.r_zx, self.s_xx, self.r_xx, self.s_zz, self.r_zz = sems
+
+    def rows(self, last, way, parity):
+        if not last:
+            return pl.ds(0, SHARD)
+        return pl.ds(0, 48) if (way + parity) % 2 == 0 else pl.ds(48, 32)
+
+    def xz(self, step, way, wait):
+        me, sign, i = self.me, 1 - 2 * way, way * 4 + step - 1
+        ref = self.wx.at[me.zn(-sign * (step if wait else step - 1)), me.x, self.rows(step == 4, way, 0)]
+        if wait:
+            arrived(ref, self.r_xz.at[i])
+        else:
+            self.send(ref, ref, self.s_xz.at[i], self.r_xz.at[i], me.at_z(sign))
+
+    def xx(self, d, step, way, wait):
+        me, sign, i = self.me, 1 - 2 * way, way * 2 + step - 1
+        ref = self.wx.at[me.zn(d), me.xn(-sign * (step if wait else step - 1)), self.rows(step == 2, way, d)]
+        if wait:
+            arrived(ref, self.r_xx.at[d, i])
+        else:
+            self.send(ref, ref, self.s_xx.at[d, i], self.r_xx.at[d, i], me.at_x(sign))
+
+    def zx(self, step, way, wait):
+        me, sign, i = self.me, 1 - 2 * way, way * 2 + step - 1
+        ref = self.wz.at[me.z, me.xn(-sign * (step if wait else step - 1)), self.rows(step == 2, way, 1)]
+        if wait:
+            arrived(ref, self.r_zx.at[i])
+        else:
+            self.send(ref, ref, self.s_zx.at[i], self.r_zx.at[i], me.at_x(sign))
+
+    def zz(self, j, step, way, wait):
+        me, sign, i = self.me, 1 - 2 * way, way * 4 + step - 1
+        ref = self.wz.at[me.zn(-sign * (step if wait else step - 1)), me.xn(j), self.rows(step == 4, way, j)]
+        if wait:
+            arrived(ref, self.r_zz.at[j, i])
+        else:
+            self.send(ref, ref, self.s_zz.at[j, i], self.r_zz.at[j, i], me.at_z(sign))
+
+    def start(self):
+        for way in (0, 1):
+            self.xz(1, way, False)
+            self.zx(1, way, False)
+        for way in (0, 1):
+            self.xx(0, 1, way, False)
+            self.zz(0, 1, way, False)
+
+    def event(self, kind, i, step, way):
+        if kind == 0:
+            self.xz(step, way, True)
+            if step < 4:
+                self.xz(step + 1, way, False)
+                for out in (0, 1):
+                    self.xx(step if way else NZ - step, 1, out, False)
+        elif kind == 1:
+            self.xx(i, step, way, True)
+            if step == 1:
+                self.xx(i, 2, way, False)
+        elif kind == 2:
+            self.zx(step, way, True)
+            if step == 1:
+                self.zx(2, way, False)
+                for out in (0, 1):
+                    self.zz(1 if way else 3, 1, out, False)
+        else:
+            self.zz(i, step, way, True)
+            if step < 4:
+                self.zz(i, step + 1, way, False)
+        self.seen.add((kind, step, way))
+        for both, ready in ((0, 4), (2, 2)):
+            if kind == both and step == ready and (kind, step, 1 - way) in self.seen:
+                for out in (0, 1):
+                    if kind == 0:
+                        self.xx(4, 1, out, False)
+                    else:
+                        self.zz(2, 1, out, False)
 
 
 def onehot(hit):
@@ -95,12 +199,12 @@
 def attend_kernel(
     hidden_hbm, w_hbm, group_hbm, blocks, prefix, table_hbm, pool, out,
     hidden, w, group, table,
-    wx, wz, ab, nb, ssq_s, ssq_r, cs, cr,
+    qx, qz, kx, vz, ab, nb, ssq_s, ssq_r, cs, cb, cr,
     un, pref, pages, pick_send, pick_in, pick_out, pick_home,
     q_send, q_recv, o_send, o_recv, local_out, local_lse, gathered,
     s_ss, r_ss, s_a, r_a, s_b, r_b, s_c, r_c,
-    s_xz, r_xz, s_zx, r_zx, s_xx, r_xx, s_zz, r_zz,
     load_sem, s_q, r_q, s_o, r_o,
+    *gather_sems,
 ):
     me = Place()
     send = Sends()
@@ -127,8 +231,25 @@
     load_pages.start()
 
     load_w.wait()
-    wx[z, x] = w[:, :XC]
-    wz[z, x] = w[:, XC:]
+    start = 0
+    for part, width in ((qx, QX), (qz, QZ), (kx, KX), (vz, VZ)):
+        part[z, x] = w[:, start : start + width]
+        start += width
+    q_recv[...] = jnp.zeros_like(q_recv)
+    o_recv[...] = jnp.zeros_like(o_recv)
+    pl.semaphore_wait(barrier, len(peers))
+
+    g1 = Gather(me, send, qx, qz, gather_sems[:8])
+    g2 = Gather(me, send, kx, vz, gather_sems[8:])
+    g1.start()
+
+    def run(stretch):
+        for code in ORDER[stretch]:
+            group_of, kind, i, step = code // 1024, code % 1024 // 256, code % 256 // 16, code % 16 // 2
+            (g1, g2)[group_of].event(kind, i, step, code % 2)
+            if group_of == 0 and (kind, step, code % 2) == (0, 3, 0):
+                g2.start()
+
     load_hidden.wait()
     total = jnp.zeros((ROWS, HD), jnp.float32)
     for b in range(10):
@@ -137,6 +258,8 @@
     total = jnp.sum(total, axis=-1, keepdims=True)
     flat = jnp.broadcast_to(total, (ROWS, ROWS)).T[:8]
     ssq_s[...] = flat
+    for k, tp in ((1, me.t1), (2, me.t2), (3, me.t3)):
+        send(ssq_s, ssq_r.at[k], s_ss.at[k], r_ss.at[k], me.other(False, tp))
     load_group.wait()
     load_table.wait()
     slot = lax.shift_right_logical(group[...], 1) * TILE + jnp.bitwise_and(group[...], 1) * REPEAT
@@ -176,72 +299,6 @@
             return carry
 
         lax.fori_loop(0, ROWS, one, 0, unroll=8)
-
-    pl.semaphore_wait(barrier, len(peers))
-
-    for k, tp in ((1, me.t1), (2, me.t2), (3, me.t3)):
-        send(ssq_s, ssq_r.at[k], s_ss.at[k], r_ss.at[k], me.other(False, tp))
-
-    XH = XC // 2
-    ZH = 256
-    full_x, half_x = pl.ds(0, XC), (pl.ds(0, XH), pl.ds(XH, XC - XH))
-    full_z, half_z = pl.ds(0, ZC), (pl.ds(0, ZH), pl.ds(ZH, ZC - ZH))
-
-    def xz_send(step, way):
-        sign = 1 - 2 * way
-        cols = full_x if step < 4 else half_x[way]
-        ref = wx.at[me.zn(-sign * (step - 1)), x, :, cols]
-        i = way * 4 + step - 1
-        send(ref, ref, s_xz.at[i], r_xz.at[i], me.at_z(sign))
-
-    def xz_wait(step, way):
-        sign = 1 - 2 * way
-        cols = full_x if step < 4 else half_x[way]
-        arrived(wx.at[me.zn(-sign * step), x, :, cols], r_xz.at[way * 4 + step - 1])
-
-    def xx_send(d, step, way):
-        sign = 1 - 2 * way
-        cols = full_x if step == 1 else half_x[way]
-        ref = wx.at[me.zn(d), me.xn(-sign * (step - 1)), :, cols]
-        i = way * 2 + step - 1
-        send(ref, ref, s_xx.at[d, i], r_xx.at[d, i], me.at_x(sign))
-
-    def xx_wait(d, step, way):
-        sign = 1 - 2 * way
-        cols = full_x if step == 1 else half_x[way]
-        arrived(wx.at[me.zn(d), me.xn(-sign * step), :, cols], r_xx.at[d, way * 2 + step - 1])
-
-    def zx_send(step, way):
-        sign = 1 - 2 * way
-        cols = full_z if step == 1 else half_z[way]
-        ref = wz.at[z, me.xn(-sign * (step - 1)), :, cols]
-        i = way * 2 + step - 1
-        send(ref, ref, s_zx.at[i], r_zx.at[i], me.at_x(sign))
-
-    def zx_wait(step, way):
-        sign = 1 - 2 * way
-        cols = full_z if step == 1 else half_z[way]
-        arrived(wz.at[z, me.xn(-sign * step), :, cols], r_zx.at[way * 2 + step - 1])
-
-    def zz_send(j, step, way):
-        sign = 1 - 2 * way
-        cols = full_z if step < 4 else half_z[way]
-        ref = wz.at[me.zn(-sign * (step - 1)), me.xn(j), :, cols]
-        i = way * 4 + step - 1
-        send(ref, ref, s_zz.at[j, i], r_zz.at[j, i], me.at_z(sign))
-
-    def zz_wait(j, step, way):
-        sign = 1 - 2 * way
-        cols = full_z if step < 4 else half_z[way]
-        arrived(wz.at[me.zn(-sign * step), me.xn(j), :, cols], r_zz.at[j, way * 4 + step - 1])
-
-    both = (0, 1)
-    for way in both:
-        xz_send(1, way)
-        zx_send(1, way)
-    for way in both:
-        xx_send(0, 1, way)
-        zz_send(0, 1, way)
 
     ssum = flat
     for k in (1, 2, 3):
@@ -270,88 +327,14 @@
     sibling = me.other(False, me.t1)
     send(nb.at[y], ab.at[t, y], s_b.at[3], r_b.at[3], sibling)
 
-    def x_first():
-        for way in both:
-            zx_wait(1, way)
-            zx_send(2, way)
-        for j in (3, 1):
-            for way in both:
-                zz_send(j, 1, way)
-
-    def xz_round(step):
-        for way in both:
-            xz_wait(step, way)
-            if step < 4:
-                xz_send(step + 1, way)
-        if step < 4:
-            for d in (NZ - step, step):
-                for way in both:
-                    xx_send(d, 1, way)
-        else:
-            for way in both:
-                xx_send(4, 1, way)
-
-    def zz_round(j, step):
-        for way in both:
-            zz_wait(j, step, way)
-            if step < 4:
-                zz_send(j, step + 1, way)
-
-    def xx_round(d):
-        for way in both:
-            xx_wait(d, 1, way)
-            xx_send(d, 2, way)
-
-    build_send()
-    x_first()
-    xz_round(1)
-    build_in()
-    for way in both:
-        zx_wait(2, way)
-    for way in both:
-        zz_send(2, 1, way)
-    xz_round(2)
-    xx_round(0)
-    zz_round(0, 1)
-    for i, (tp, yy) in enumerate(((t, me.ty), (me.t2, y), (me.t2, me.ty))):
-        arrived(ab.at[tp, yy], r_a.at[i])
-        send(ab.at[tp, yy], ab.at[tp, yy], s_b.at[i], r_b.at[i], sibling)
-    build_out()
-    xz_round(3)
-    zz_round(3, 1)
-    zz_round(1, 1)
-    xx_round(7)
-    xx_round(1)
-    xz_round(4)
-    zz_round(2, 1)
-    zz_round(0, 2)
-    xx_round(6)
-    xx_round(2)
-    build_home()
-    zz_round(3, 2)
-    zz_round(1, 2)
-    zz_round(2, 2)
-    xx_round(5)
-    xx_round(3)
-    zz_round(0, 3)
-    zz_round(3, 3)
-    zz_round(1, 3)
-    zz_round(2, 3)
-    xx_round(4)
-    gather_pages()
-    for i, (tp, yy) in enumerate(
-        ((me.t1, me.ty), (me.t3, y), (me.t3, me.ty), (me.t1, y))
-    ):
-        arrived(ab.at[tp, yy], r_b.at[i])
-    for d in range(NZ):
-        for way in both:
-            xx_wait(d, 2, way)
-    for j in range(NX):
-        zz_round(j, 4)
+    def pass_rows():
+        for i, (tp, yy) in enumerate(((t, me.ty), (me.t2, y), (me.t2, me.ty))):
+            arrived(ab.at[tp, yy], r_a.at[i])
+            send(ab.at[tp, yy], ab.at[tp, yy], s_b.at[i], r_b.at[i], sibling)
 
     partner = me.other(True, t)
-    for i, (start, width) in enumerate(CHUNKS):
-        src, at = (wx, start) if start < XC else (wz, start - XC)
+
+    def product(i, src, at, width):
         acc = jnp.zeros((2 * ROWS, width), jnp.float32)
         for tp in range(4):
             acc += jnp.dot(
@@ -360,32 +343,66 @@
                 preferred_element_type=jnp.float32,
             )
         cs[i, :, :, :width] = acc.reshape(2, ROWS, width)
+        cb[i, :, :width] = cs[i, me.ty, :, :width].astype(jnp.bfloat16)
         send(
-            cs.at[i, me.ty, :, pl.ds(0, width)], cr.at[i, :, pl.ds(0, width)],
+            cb.at[i, :, pl.ds(0, width)], cr.at[i, :, pl.ds(0, width)],
             s_c.at[i], r_c.at[i], partner,
         )
-    for i, (start, width) in enumerate(CHUNKS):
+
+    def total_of(i, start, width):
         arrived(cr.at[i, :, pl.ds(0, width)], r_c.at[i])
-        un[:, start : start + width] = (cs[i, y, :, :width] + cr[i, :, :width]).astype(jnp.bfloat16)
+        un[:, start : start + width] = (cs[i, y, :, :width] + cr[i, :, :width].astype(jnp.float32)).astype(jnp.bfloat16)
+
+    run(0)
+    build_send()
+    run(1)
+    build_in()
+    pass_rows()
+    run(2)
+    build_out()
+    run(3)
+    for i, (tp, yy) in enumerate(
+        ((me.t1, me.ty), (me.t3, y), (me.t3, me.ty), (me.t1, y))
+    ):
+        arrived(ab.at[tp, yy], r_b.at[i])
+    product(2, qz, 0, 256)
+    product(0, qx, 0, 256)
+    product(1, qx, 256, 128)
+    build_home()
+    gather_pages()
+    run(4)
+    total_of(2, 384, 256)
+    total_of(0, 0, 256)
+    total_of(1, 256, 128)
 
     rows = jnp.concatenate([un[:, h * HD : (h + 1) * HD] for h in range(REPEAT)], axis=0)
     q_send[...] = jnp.dot(pick_send[...], rows, preferred_element_type=jnp.float32).astype(
         jnp.bfloat16
     ).reshape(N_ROLL, TILE, HD)
 
-    def exchange(src, dst, s_sem, r_sem):
-        def one(i, carry):
-            peer = lax.rem(me.r + i, N_ROLL)
-            pltpu.make_async_remote_copy(
-                src_ref=src.at[peer], dst_ref=dst.at[me.r], send_sem=s_sem, recv_sem=r_sem,
-                device_id={"roll": peer, "tp": t}, device_id_type=MESH,
-            ).start()
-            return carry
-
-        lax.fori_loop(1, N_ROLL, one, 0)
+    def exchange(src, dst, rows, s_sem, r_sem):
+        here = y * NX + x
+        for dz in (4, 3, 5, 2, 6, 1, 7, 0):
+
+            def one(i, carry):
+                peer = me.zn(dz) * (NX * NY) + lax.rem(here + i, NX * NY)
+                pltpu.make_async_remote_copy(
+                    src_ref=src.at[peer, pl.ds(0, rows)], dst_ref=dst.at[me.r, pl.ds(0, rows)],
+                    send_sem=s_sem, recv_sem=r_sem,
+                    device_id={"roll": peer, "tp": t}, device_id_type=MESH,
+                ).start()
+                return carry
+
+            lax.fori_loop(1 if dz == 0 else 0, NX * NY, one, 0)
         dst[me.r] = src[me.r]
 
-    exchange(q_send, q_recv, s_q, r_q)
+    def all_of(ref, rows, sem):
+        arrived(ref.at[pl.ds(0, N_ROLL - 1), pl.ds(0, rows)], sem)
+
+    exchange(q_send, q_recv, 10, s_q, r_q)
+    run(5)
+    product(3, kx, 0, 128)
+    product(4, vz, 0, 128)
 
     def local_block(b, carry):
         at = pl.ds(pl.multiple_of(b * SB, SB), SB)
@@ -416,10 +433,8 @@
             local_lse[h, at, :] = lse[h * SB : (h + 1) * SB]
         return carry
 
-    lax.fori_loop(0, ROWS // SB, local_block, 0)
-
     load_prefix.wait()
-    arrived(q_recv.at[pl.ds(0, N_ROLL - 1)], r_q)
+    all_of(q_recv, 10, r_q)
     came = q_recv[...].reshape(N_ROLL * TILE, HD)
     outs, marks = [], []
     per = REPEAT * N_ROLL
@@ -449,9 +464,11 @@
     o_send[...] = jnp.dot(pick_out[...], stacked, preferred_element_type=jnp.float32).astype(
         jnp.bfloat16
     ).reshape(N_ROLL, TILE, HD)
-    exchange(o_send, o_recv, s_o, r_o)
-
-    arrived(o_recv.at[pl.ds(0, N_ROLL - 1)], r_o)
+    exchange(o_send, o_recv, 12, s_o, r_o)
+    total_of(3, 640, 128)
+    total_of(4, 768, 128)
+    lax.fori_loop(0, ROWS // SB, local_block, 0)
+    all_of(o_recv, 12, r_o)
     back = jnp.dot(
         pick_home[...], o_recv[...].reshape(N_ROLL * TILE, HD), preferred_element_type=jnp.float32
     )
@@ -469,8 +486,8 @@
         mixed = (ep * back[h * ROWS : (h + 1) * ROWS] + el * local_out[h]) / (ep + el)
         out[:, h * HD : (h + 1) * HD] = mixed.astype(jnp.bfloat16)
 
-    arrived(q_send.at[pl.ds(0, N_ROLL - 1)], s_q)
-    arrived(o_send.at[pl.ds(0, N_ROLL - 1)], s_o)
+    all_of(q_send, 10, s_q)
+    all_of(o_send, 12, s_o)
     send.finish()
 
 
@@ -483,8 +500,11 @@
     hbm = pl.BlockSpec(memory_space=pl.ANY)
     bf16, f32 = jnp.bfloat16, jnp.float32
     sems = []
-    for shape in ((4,), (3,), (4,), (4,), (8,), (4,), (8, 4), (4, 8)):
+    for shape in ((4,), (3,), (4,), (5,)):
         sems += [dma(shape), dma(shape)]
+    gather_sems = []
+    for shape in ((8,), (4,), (8, 4), (4, 8)) * 2:
+        gather_sems += [dma(shape), dma(shape)]
     tiles = pltpu.VMEM((N_ROLL, TILE, HD), bf16)
     return pl.pallas_call(
         attend_kernel,
@@ -493,18 +513,18 @@
         out_specs=vmem,
         scratch_shapes=[
             pltpu.VMEM((ROWS, 10 * HD), bf16),
-            pltpu.VMEM((SHARD, XC + ZC), bf16),
+            pltpu.VMEM((SHARD, QX + QZ + KX + VZ), bf16),
             pltpu.VMEM((1, ROWS), jnp.int32),
             pltpu.SMEM((SPAGES, ROWS), jnp.int32),
-            pltpu.VMEM((NZ, NX, SHARD, XC), bf16),
-            pltpu.VMEM((NZ, NX, SHARD, ZC), bf16),
+            *(pltpu.VMEM((NZ, NX, SHARD, width), bf16) for width in (QX, QZ, KX, VZ)),
             pltpu.VMEM((4, 2, ROWS, 640), bf16),
             pltpu.VMEM((2, ROWS, 640), bf16),
             pltpu.VMEM((8, ROWS), f32),
             pltpu.VMEM((4, 8, ROWS), f32),
-            pltpu.VMEM((4, 2, ROWS, 256), f32),
-            pltpu.VMEM((4, ROWS, 256), f32),
-            pltpu.VMEM((ROWS, XC + ZC), bf16),
+            pltpu.VMEM((5, 2, ROWS, 256), f32),
+            pltpu.VMEM((5, ROWS, 256), bf16),
+            pltpu.VMEM((5, ROWS, 256), bf16),
+            pltpu.VMEM((ROWS, QX + QZ + KX + VZ), bf16),
             pltpu.VMEM(prefix_kv.shape, bf16),
             pltpu.VMEM(suffix_pool.shape, bf16),
             pltpu.VMEM((N_ROLL * TILE, REPEAT * ROWS), bf16),
@@ -517,6 +537,7 @@
             pltpu.VMEM((ROWS, SPAGES, PAGE, 2 * HD), bf16),
             *sems,
             dma((6,)), dma, dma, dma, dma,
+            *gather_sems,
         ],
         compiler_params=pltpu.CompilerParams(
             collective_id=0, has_side_effects=True, vmem_limit_bytes=62 * 1024 * 1024

time: 76.8 us -> 68.5 us (0.89)
  Pallas kernels: 75 us -> 66.7 us
    pallas_call x1, Pallas kernels: 75 us -> 66.7 us  [per_device(): pl.pallas_call(attend_kernel, out_shape=jax.ShapeDtypeStruct((ROWS, REPEA...]
where the time goes in v4:
time: 68.5 us; the launch traced here: 68.3 us
  Pallas kernels  66.7 us (97%)
  local copies, waits for them, and re-layouts  1.6 us (2%)
    pallas_call x1, Pallas kernels, per_device(): pl.pallas_call(attend_kernel, out_shape=jax.ShapeDtypeStruct((ROWS, REPEA...  66.7 us
    unnamed x1, local copies, waits for them, and re-layouts  1.6 us

profile of v4, /device:TPU:8, one launch (start us, length us, event | category | flops | bytes accessed | tf_op | source)
XLA Modules:
  0.0 68.3 jit_solution(892616527817924582)
XLA Ops:
  0.0 66.7 %shard_map.73 = bf16[128,640]{1,0:T(8,128)(2,1)} custom-call(bf16[128,1280]{1,0:T(8,128)(2,1)} %hidden_hbm.1, bf16[80,896]{1,0:T(8,128)(2,1)} %w_hbm.1, s32[1,128]{1,0:T(1,128)} %bitcast.3, s32[2]{0:T(128)} %blocks.1, bf16[2,512,256]{2,1,0:T(8,128)(2,1)} %prefix.1, s32[2,128]{1,0:T(2,128)} %bitcast.2, bf16[256,16,256]{2,1,0:T(8,128)(2,1)} %pool.1), custom_call_target="tpu_custom_call" | custom-call | tf_op jit(solution)/shard_map/pallas_call | solution.py:509
  66.7 1.6 %copy.9 = bf16[128,640]{1,0:T(8,128)(2,1)} copy(bf16[128,640]{1,0:T(8,128)(2,1)} %shard_map.73) | data formatting | bytes 327680

commit v5 on v4

--- a/solution.py
+++ b/solution.py
@@ -28,29 +28,42 @@
 MESH = pl.DeviceIdType.MESH
 ORDER = (
     (
-        514, 515, 2, 3, 770, 771, 258, 259, 516, 517, 818, 819,
-    ),
-    (
-        370, 786, 787, 371, 274, 4, 5, 275, 260, 261, 772, 773, 372, 802, 803, 373, 820, 821,
-        276,
-    ),
-    (
-        788, 789, 355, 354, 6, 7, 291, 290, 774, 775, 277, 357, 804, 805, 356, 822,
-    ),
-    (
-        823, 790, 791, 338, 339, 1027, 1282, 1283, 8, 1795, 1538, 1539, 1026, 9, 1794, 777, 776, 306,
-        307, 807, 293, 806, 292, 825, 824, 340, 341, 793, 792, 1298, 1299, 1029, 1842, 1285, 1284, 1797,
-        1810, 1843, 1028, 1811, 1796, 323, 322, 809, 1540, 1541, 808, 1394, 1395, 308, 1300, 1031, 309, 1844,
-        1301, 1314, 1799, 1812, 1315, 1378, 1845, 1030, 1379, 1813, 1798, 325, 324,
-    ),
-    (
-        1827, 1826, 1396, 1397, 1033, 1330, 1331, 1801, 1846, 1316, 1317, 1814, 1380, 1847, 1032, 1363, 1362, 1381,
-        1800, 1815, 1829, 1828, 1332,
-    ),
-    (
-        1333, 1848, 1816, 1849, 1346, 1347, 1364, 1817, 1365, 1831, 1830, 1349, 1348, 1833, 1832,
+        16, 17, 528, 529, 272, 273, 784, 785,
+    ),
+    (
+        1040, 1041, 1552, 1553, 1296, 1297, 1808, 1809, 2576, 2577, 522, 515, 880, 881, 2064, 2065, 496, 497,
+        18, 19, 304, 305, 816, 817, 2320, 2321, 2832, 2833, 3088, 3089, 3600, 3601, 258, 267, 3344, 3345,
+        3856, 3857,
+    ),
+    (
+        1539, 1546, 1521, 786, 787, 1520, 2570, 2563, 848, 849, 1329, 2066, 2067, 464, 465, 20, 21, 336,
+        337, 2928, 2929, 2864, 2865, 882, 883, 2544, 2545, 2352, 2353, 818, 819, 490,
+    ),
+    (
+        2315, 483, 2306, 2896, 2897, 3594, 3587, 298, 850, 851, 1328, 291, 2834, 2835, 789, 788, 2068, 2069,
+        432, 6, 15, 433, 368, 369, 2512, 2513, 2384, 2385, 450, 2538, 2930, 2931, 2866, 2867, 885, 884,
+        821, 820, 459,
+    ),
+    (
+        2346, 2531, 3568, 3569, 3376, 3377, 2898, 2899, 853, 852, 2339, 2054, 2063, 400, 401, 1043, 322, 331,
+        1042, 1905, 1904, 2836, 2837, 783, 774, 1841, 1282, 1840, 2480, 2481, 2416, 2417, 419, 426, 362, 355,
+        1514, 1507, 1322, 2498, 2507, 2932, 2933, 2868, 2869, 878, 871, 814, 807, 1873, 1872, 2900, 2901, 847,
+        838, 1811, 2831, 1810, 2448, 2449, 386, 395, 2822, 1315, 1291, 2379, 3090, 3091, 1045, 1489, 1488, 1044,
+        1361, 1360, 2370, 2474, 2467, 2926, 2919, 2410, 2862, 3330, 2855, 2403, 3562, 3952, 3953, 3888, 3889, 1906,
+        1907, 1842, 1843, 3370, 3555, 2895, 2886, 2443, 2434,
+    ),
+    (
+        3920, 3921, 1874, 1875, 3092, 3093, 1030, 1039, 1456, 1457, 1392, 1393, 3536, 3537, 3408, 3409, 3858, 3859,
+        1474, 1483, 1355, 1346, 1812, 1813, 3363, 3339, 3954, 3955, 3890, 3891, 1908, 1909, 1844, 1845, 3922, 3923,
+        1876, 1877, 3078, 3087, 1424, 1425,
+    ),
+    (
+        3504, 3505, 3440, 3441, 3860, 3861, 1450, 1443, 1386, 1379, 1798, 1807, 3531, 3522, 3403, 3394, 3956, 3957,
+        3892, 3893, 1902, 1895, 1838, 1831, 3472, 3473, 1410, 1419, 3924, 3925, 1862, 1871, 3498, 3855, 3491, 3846,
+        3434, 3427, 3950, 3943, 3886, 3467, 3879, 3458, 3919, 3910,
     ),
 )
+PIECES = ((0, 48), (48, 32), (0, 80))
 
 
 class Place:
@@ -85,21 +98,10 @@
         return {"roll": self.roll(self.z, y, self.x), "tp": tp}
 
 
-class Sends:
-    def __init__(self):
-        self.copies = []
-
-    def __call__(self, src, dst, send, recv, device):
-        copy = pltpu.make_async_remote_copy(
-            src_ref=src, dst_ref=dst, send_sem=send, recv_sem=recv,
-            device_id=device, device_id_type=MESH,
-        )
-        copy.start()
-        self.copies.append(copy)
-
-    def finish(self):
-        for copy in self.copies:
-            copy.wait_send()
+def send(src, dst, s_sem, r_sem, device):
+    pltpu.make_async_remote_copy(
+        src_ref=src, dst_ref=dst, send_sem=s_sem, recv_sem=r_sem, device_id=device, device_id_type=MESH
+    ).start()
 
 
 def arrived(ref, sem):
@@ -107,85 +109,40 @@
 
 
 class Gather:
-    def __init__(self, me, send, wx, wz, sems):
-        self.me, self.send, self.wx, self.wz = me, send, wx, wz
-        self.seen = set()
-        self.s_xz, self.r_xz, self.s_zx, self.r_zx, self.s_xx, self.r_xx, self.s_zz, self.r_zz = sems
-
-    def rows(self, last, way, parity):
-        if not last:
-            return pl.ds(0, SHARD)
-        return pl.ds(0, 48) if (way + parity) % 2 == 0 else pl.ds(48, 32)
-
-    def xz(self, step, way, wait):
-        me, sign, i = self.me, 1 - 2 * way, way * 4 + step - 1
-        ref = self.wx.at[me.zn(-sign * (step if wait else step - 1)), me.x, self.rows(step == 4, way, 0)]
-        if wait:
-            arrived(ref, self.r_xz.at[i])
-        else:
-            self.send(ref, ref, self.s_xz.at[i], self.r_xz.at[i], me.at_z(sign))
-
-    def xx(self, d, step, way, wait):
-        me, sign, i = self.me, 1 - 2 * way, way * 2 + step - 1
-        ref = self.wx.at[me.zn(d), me.xn(-sign * (step if wait else step - 1)), self.rows(step == 2, way, d)]
-        if wait:
-            arrived(ref, self.r_xx.at[d, i])
-        else:
-            self.send(ref, ref, self.s_xx.at[d, i], self.r_xx.at[d, i], me.at_x(sign))
-
-    def zx(self, step, way, wait):
-        me, sign, i = self.me, 1 - 2 * way, way * 2 + step - 1
-        ref = self.wz.at[me.z, me.xn(-sign * (step if wait else step - 1)), self.rows(step == 2, way, 1)]
-        if wait:
-            arrived(ref, self.r_zx.at[i])
-        else:
-            self.send(ref, ref, self.s_zx.at[i], self.r_zx.at[i], me.at_x(sign))
-
-    def zz(self, j, step, way, wait):
-        me, sign, i = self.me, 1 - 2 * way, way * 4 + step - 1
-        ref = self.wz.at[me.zn(-sign * (step if wait else step - 1)), me.xn(j), self.rows(step == 4, way, j)]
-        if wait:
-            arrived(ref, self.r_zz.at[j, i])
-        else:
-            self.send(ref, ref, self.s_zz.at[j, i], self.r_zz.at[j, i], me.at_z(sign))
-
-    def start(self):
-        for way in (0, 1):
-            self.xz(1, way, False)
-            self.zx(1, way, False)
-        for way in (0, 1):
-            self.xx(0, 1, way, False)
-            self.zz(0, 1, way, False)
-
-    def event(self, kind, i, step, way):
-        if kind == 0:
-            self.xz(step, way, True)
-            if step < 4:
-                self.xz(step + 1, way, False)
-                for out in (0, 1):
-                    self.xx(step if way else NZ - step, 1, out, False)
-        elif kind == 1:
-            self.xx(i, step, way, True)
-            if step == 1:
-                self.xx(i, 2, way, False)
-        elif kind == 2:
-            self.zx(step, way, True)
-            if step == 1:
-                self.zx(2, way, False)
-                for out in (0, 1):
-                    self.zz(1 if way else 3, 1, out, False)
-        else:
-            self.zz(i, step, way, True)
-            if step < 4:
-                self.zz(i, step + 1, way, False)
-        self.seen.add((kind, step, way))
-        for both, ready in ((0, 4), (2, 2)):
-            if kind == both and step == ready and (kind, step, 1 - way) in self.seen:
-                for out in (0, 1):
-                    if kind == 0:
-                        self.xx(4, 1, out, False)
-                    else:
-                        self.zz(2, 1, out, False)
+    def __init__(self, me, wx, wz, s_sem, r_sem):
+        self.me, self.wx, self.wz, self.s_sem, self.r_sem = me, wx, wz, s_sem, r_sem
+        self.sems, self.waited = {}, set()
+
+    def step(self, code):
+        me, wait, key = self.me, code >= 2048, code % 1024
+        kind, i, rows, hop, way = key >> 8, key >> 5 & 7, PIECES[key >> 3 & 3], (key >> 1 & 3) + 1, key & 1
+        sign = 1 - 2 * way
+        back = -sign * (hop if wait else hop - 1)
+        ref, z, x = (
+            (self.wx, me.zn(back), me.x),
+            (self.wx, me.zn(i), me.xn(back)),
+            (self.wz, me.z, me.xn(back)),
+            (self.wz, me.zn(back), me.xn(i)),
+        )[kind]
+        ref = ref.at[z * NX + x, pl.ds(*rows)]
+        shape = (kind, hop, (min(i, NZ - i), min(i, NX - i))[kind // 2])
+        final = (1, 2, 0) if (kind, hop) == (1, 2) else (3, 4, 0) if (kind, hop) == (3, 4) else None
+        sem = self.sems.setdefault(final or shape, len(self.sems))
+        if not wait:
+            to = me.at_z(sign) if kind in (0, 3) else me.at_x(sign)
+            send(ref, ref, self.s_sem.at[kind // 2], self.r_sem.at[sem], to)
+        elif not final and shape not in self.waited:
+            self.waited.add(shape)
+            count = 1 if (kind, hop) in ((0, 4), (2, 2)) else 4 if shape[2] and 2 * shape[2] != (NZ, NX)[kind // 2] else 2
+            arrived((self.wx, self.wz)[kind // 2].at[pl.ds(0, count)], self.r_sem.at[sem])
+
+    def finish(self):
+        arrived(self.wx.at[pl.ds(0, NZ)], self.r_sem.at[self.sems[1, 2, 0]])
+        arrived(self.wz.at[pl.ds(0, NX)], self.r_sem.at[self.sems[3, 4, 0]])
+
+    def sent(self):
+        arrived(self.wx.at[pl.ds(0, NZ * NX - 1)], self.s_sem.at[0])
+        arrived(self.wz.at[pl.ds(0, NZ * NX - 1)], self.s_sem.at[1])
 
 
 def onehot(hit):
@@ -207,7 +164,6 @@
     *gather_sems,
 ):
     me = Place()
-    send = Sends()
     x, y, z, t = me.x, me.y, me.z, me.t
     barrier = pltpu.get_barrier_semaphore()
     peers = [
@@ -233,23 +189,34 @@
     load_w.wait()
     start = 0
     for part, width in ((qx, QX), (qz, QZ), (kx, KX), (vz, VZ)):
-        part[z, x] = w[:, start : start + width]
+        part[z * NX + x] = w[:, start : start + width]
         start += width
+    def build_in():
+        for i in range(2 * REPEAT):
+            target = iota((N_ROLL, N_ROLL * TILE), 0) * TILE + i
+            pick_in[i * N_ROLL : (i + 1) * N_ROLL, :] = onehot(iota((N_ROLL, N_ROLL * TILE), 1) == target)
+
+    def build_out():
+        for i in range(2 * REPEAT):
+            lane = iota((N_ROLL * TILE, ROWS), 1) + (i % REPEAT) * ROWS
+            row = lax.shift_right_logical(lane, 6) if i < REPEAT else 2 * REPEAT
+            target = jnp.bitwise_and(lane, N_ROLL - 1) * TILE + row
+            pick_out[:, i * ROWS : (i + 1) * ROWS] = onehot(iota((N_ROLL * TILE, ROWS), 0) == target)
+
+    build_in()
+    build_out()
     q_recv[...] = jnp.zeros_like(q_recv)
     o_recv[...] = jnp.zeros_like(o_recv)
     pl.semaphore_wait(barrier, len(peers))
 
-    g1 = Gather(me, send, qx, qz, gather_sems[:8])
-    g2 = Gather(me, send, kx, vz, gather_sems[8:])
-    g1.start()
+    g1 = Gather(me, qx, qz, *gather_sems[:2])
+    g2 = Gather(me, kx, vz, *gather_sems[2:])
 
     def run(stretch):
         for code in ORDER[stretch]:
-            group_of, kind, i, step = code // 1024, code % 1024 // 256, code % 256 // 16, code % 16 // 2
-            (g1, g2)[group_of].event(kind, i, step, code % 2)
-            if group_of == 0 and (kind, step, code % 2) == (0, 3, 0):
-                g2.start()
-
+            (g1, g2)[code >> 10 & 1].step(code)
+
+    run(0)
     load_hidden.wait()
     total = jnp.zeros((ROWS, HD), jnp.float32)
     for b in range(10):
@@ -259,7 +226,7 @@
     flat = jnp.broadcast_to(total, (ROWS, ROWS)).T[:8]
     ssq_s[...] = flat
     for k, tp in ((1, me.t1), (2, me.t2), (3, me.t3)):
-        send(ssq_s, ssq_r.at[k], s_ss.at[k], r_ss.at[k], me.other(False, tp))
+        send(ssq_s, ssq_r.at[k], s_ss, r_ss, me.other(False, tp))
     load_group.wait()
     load_table.wait()
     slot = lax.shift_right_logical(group[...], 1) * TILE + jnp.bitwise_and(group[...], 1) * REPEAT
@@ -269,18 +236,6 @@
     def build_send():
         for h in range(REPEAT):
             pick_send[:, h * ROWS : (h + 1) * ROWS] = onehot(iota((N_ROLL * TILE, ROWS), 0) == slot + h)
-
-    def build_in():
-        for i in range(2 * REPEAT):
-            target = iota((N_ROLL, N_ROLL * TILE), 0) * TILE + i
-            pick_in[i * N_ROLL : (i + 1) * N_ROLL, :] = onehot(iota((N_ROLL, N_ROLL * TILE), 1) == target)
-
-    def build_out():
-        for i in range(2 * REPEAT):
-            lane = iota((N_ROLL * TILE, ROWS), 1) + (i % REPEAT) * ROWS
-            row = lax.shift_right_logical(lane, 6) if i < REPEAT else 2 * REPEAT
-            target = jnp.bitwise_and(lane, N_ROLL - 1) * TILE + row
-            pick_out[:, i * ROWS : (i + 1) * ROWS] = onehot(iota((N_ROLL * TILE, ROWS), 0) == target)
 
     def build_home():
         for b in range(N_ROLL * TILE // ROWS):
@@ -301,8 +256,8 @@
         lax.fori_loop(0, ROWS, one, 0, unroll=8)
 
     ssum = flat
+    arrived(ssq_r.at[pl.ds(1, 3)], r_ss)
     for k in (1, 2, 3):
-        arrived(ssq_r.at[k], r_ss.at[k])
         ssum += ssq_r[k]
     scale = lax.rsqrt(ssum / D + 1e-06)
     scale = jnp.broadcast_to(scale[:1], (ROWS, ROWS)).T
@@ -320,60 +275,54 @@
     for side in range(2):
         for b in range(5):
             nb[side, :, b * HD : (b + 1) * HD] = sides[side][b].astype(jnp.bfloat16)
-    ab[t, y] = nb[y]
-    send(nb.at[me.ty], ab.at[t, y], s_a.at[0], r_a.at[0], me.other(True, t))
-    send(nb.at[y], ab.at[t, y], s_a.at[1], r_a.at[1], me.other(False, me.t2))
-    send(nb.at[me.ty], ab.at[t, y], s_a.at[2], r_a.at[2], me.other(True, me.t2))
+    ab[2 * t + y] = nb[y]
+    send(nb.at[me.ty], ab.at[2 * t + y], s_a, r_a, me.other(True, t))
+    send(nb.at[y], ab.at[2 * t + y], s_a, r_a, me.other(False, me.t2))
+    send(nb.at[me.ty], ab.at[2 * t + y], s_a, r_a, me.other(True, me.t2))
     sibling = me.other(False, me.t1)
-    send(nb.at[y], ab.at[t, y], s_b.at[3], r_b.at[3], sibling)
+    send(nb.at[y], ab.at[2 * t + y], s_b, r_b, sibling)
 
     def pass_rows():
-        for i, (tp, yy) in enumerate(((t, me.ty), (me.t2, y), (me.t2, me.ty))):
-            arrived(ab.at[tp, yy], r_a.at[i])
-            send(ab.at[tp, yy], ab.at[tp, yy], s_b.at[i], r_b.at[i], sibling)
+        arrived(ab.at[pl.ds(0, 3)], r_a)
+        for row in (2 * t + me.ty, 2 * me.t2 + y, 2 * me.t2 + me.ty):
+            send(ab.at[row], ab.at[row], s_b, r_b, sibling)
 
     partner = me.other(True, t)
 
-    def product(i, src, at, width):
+    def product(block, src, at, width, r_sem):
         acc = jnp.zeros((2 * ROWS, width), jnp.float32)
         for tp in range(4):
             acc += jnp.dot(
-                ab[tp].reshape(2 * ROWS, 640),
-                src[2 * tp : 2 * tp + 2, :, :, at : at + width].reshape(640, width),
+                ab[2 * tp : 2 * tp + 2].reshape(2 * ROWS, 640),
+                src[8 * tp : 8 * tp + 8, :, at : at + width].reshape(640, width),
                 preferred_element_type=jnp.float32,
             )
-        cs[i, :, :, :width] = acc.reshape(2, ROWS, width)
-        cb[i, :, :width] = cs[i, me.ty, :, :width].astype(jnp.bfloat16)
-        send(
-            cb.at[i, :, pl.ds(0, width)], cr.at[i, :, pl.ds(0, width)],
-            s_c.at[i], r_c.at[i], partner,
-        )
-
-    def total_of(i, start, width):
-        arrived(cr.at[i, :, pl.ds(0, width)], r_c.at[i])
-        un[:, start : start + width] = (cs[i, y, :, :width] + cr[i, :, :width].astype(jnp.float32)).astype(jnp.bfloat16)
-
-    run(0)
+        blocks_of = pl.ds(block, width // HD)
+        for b in range(width // HD):
+            cs[block + b] = acc[:, b * HD : (b + 1) * HD].reshape(2, ROWS, HD)
+            cb[block + b] = cs[block + b, me.ty].astype(jnp.bfloat16)
+        send(cb.at[blocks_of], cr.at[blocks_of], s_c, r_sem, partner)
+
+    def total_of(block, count, r_sem):
+        arrived(cr.at[pl.ds(block, count)], r_sem)
+        for b in range(block, block + count):
+            un[:, b * HD : (b + 1) * HD] = (cs[b, y] + cr[b].astype(jnp.float32)).astype(jnp.bfloat16)
+
+    run(1)
+    run(2)
+    run(3)
     build_send()
-    run(1)
-    build_in()
     pass_rows()
-    run(2)
-    build_out()
-    run(3)
-    for i, (tp, yy) in enumerate(
-        ((me.t1, me.ty), (me.t3, y), (me.t3, me.ty), (me.t1, y))
-    ):
-        arrived(ab.at[tp, yy], r_b.at[i])
-    product(2, qz, 0, 256)
-    product(0, qx, 0, 256)
-    product(1, qx, 256, 128)
+    run(4)
+    g1.finish()
+    arrived(ab.at[pl.ds(0, 4)], r_b)
+    product(3, qz, 0, 256, r_c.at[0])
+    product(0, qx, 0, 256, r_c.at[0])
+    product(2, qx, 256, 128, r_c.at[0])
     build_home()
     gather_pages()
-    run(4)
-    total_of(2, 384, 256)
-    total_of(0, 0, 256)
-    total_of(1, 256, 128)
+    run(5)
+    total_of(0, 5, r_c.at[0])
 
     rows = jnp.concatenate([un[:, h * HD : (h + 1) * HD] for h in range(REPEAT)], axis=0)
     q_send[...] = jnp.dot(pick_send[...], rows, preferred_element_type=jnp.float32).astype(
@@ -400,9 +349,10 @@
         arrived(ref.at[pl.ds(0, N_ROLL - 1), pl.ds(0, rows)], sem)
 
     exchange(q_send, q_recv, 10, s_q, r_q)
-    run(5)
-    product(3, kx, 0, 128)
-    product(4, vz, 0, 128)
+    run(6)
+    g2.finish()
+    product(5, kx, 0, 128, r_c.at[1])
+    product(6, vz, 0, 128, r_c.at[1])
 
     def local_block(b, carry):
         at = pl.ds(pl.multiple_of(b * SB, SB), SB)
@@ -465,8 +415,7 @@
         jnp.bfloat16
     ).reshape(N_ROLL, TILE, HD)
     exchange(o_send, o_recv, 12, s_o, r_o)
-    total_of(3, 640, 128)
-    total_of(4, 768, 128)
+    total_of(5, 2, r_c.at[1])
     lax.fori_loop(0, ROWS // SB, local_block, 0)
     all_of(o_recv, 12, r_o)
     back = jnp.dot(
@@ -488,7 +437,12 @@
 
     all_of(q_send, 10, s_q)
     all_of(o_send, 12, s_o)
-    send.finish()
+    g1.sent()
+    g2.sent()
+    arrived(ssq_r.at[pl.ds(1, 3)], s_ss)
+    arrived(ab.at[pl.ds(0, 3)], s_a)
+    arrived(ab.at[pl.ds(0, 4)], s_b)
+    arrived(cb.at[pl.ds(0, 7)], s_c)
 
 
 def per_device(
@@ -499,12 +453,10 @@
     smem = pl.BlockSpec(memory_space=pltpu.SMEM)
     hbm = pl.BlockSpec(memory_space=pl.ANY)
     bf16, f32 = jnp.bfloat16, jnp.float32
-    sems = []
-    for shape in ((4,), (3,), (4,), (5,)):
-        sems += [dma(shape), dma(shape)]
+    sems = [dma] * 7 + [dma((2,))]
     gather_sems = []
-    for shape in ((8,), (4,), (8, 4), (4, 8)) * 2:
-        gather_sems += [dma(shape), dma(shape)]
+    for _ in range(2):
+        gather_sems += [dma((2,)), dma((22,))]
     tiles = pltpu.VMEM((N_ROLL, TILE, HD), bf16)
     return pl.pallas_call(
         attend_kernel,
@@ -516,14 +468,14 @@
             pltpu.VMEM((SHARD, QX + QZ + KX + VZ), bf16),
             pltpu.VMEM((1, ROWS), jnp.int32),
             pltpu.SMEM((SPAGES, ROWS), jnp.int32),
-            *(pltpu.VMEM((NZ, NX, SHARD, width), bf16) for width in (QX, QZ, KX, VZ)),
-            pltpu.VMEM((4, 2, ROWS, 640), bf16),
+            *(pltpu.VMEM((NZ * NX, SHARD, width), bf16) for width in (QX, QZ, KX, VZ)),
+            pltpu.VMEM((8, ROWS, 640), bf16),
             pltpu.VMEM((2, ROWS, 640), bf16),
             pltpu.VMEM((8, ROWS), f32),
             pltpu.VMEM((4, 8, ROWS), f32),
-            pltpu.VMEM((5, 2, ROWS, 256), f32),
-            pltpu.VMEM((5, ROWS, 256), bf16),
-            pltpu.VMEM((5, ROWS, 256), bf16),
+            pltpu.VMEM((7, 2, ROWS, HD), f32),
+            pltpu.VMEM((7, ROWS, HD), bf16),
+            pltpu.VMEM((7, ROWS, HD), bf16),
             pltpu.VMEM((ROWS, QX + QZ + KX + VZ), bf16),
             pltpu.VMEM(prefix_kv.shape, bf16),
             pltpu.VMEM(suffix_pool.shape, bf16),

time: 68.5 us -> 62.9 us (0.918)
  Pallas kernels: 66.7 us -> 61.2 us
    pallas_call x1, Pallas kernels: 66.7 us -> 61.2 us  [per_device(): pl.pallas_call(attend_kernel, out_shape=jax.ShapeDtypeStruct((ROWS, REPEA...]
where the time goes in v5:
time: 62.9 us; the launch traced here: 62.8 us
  Pallas kernels  61.2 us (97%)
  local copies, waits for them, and re-layouts  1.6 us (3%)
    pallas_call x1, Pallas kernels, per_device(): pl.pallas_call(attend_kernel, out_shape=jax.ShapeDtypeStruct((ROWS, REPEA...  61.2 us
    unnamed x1, local copies, waits for them, and re-layouts  1.6 us

profile of v5, /device:TPU:8, one launch (start us, length us, event | category | flops | bytes accessed | tf_op | source)
XLA Modules:
  0.0 62.8 jit_solution(1837817768520122921)
XLA Ops:
  0.0 61.2 %shard_map.73 = bf16[128,640]{1,0:T(8,128)(2,1)} custom-call(bf16[128,1280]{1,0:T(8,128)(2,1)} %hidden_hbm.1, bf16[80,896]{1,0:T(8,128)(2,1)} %w_hbm.1, s32[1,128]{1,0:T(1,128)} %bitcast.3, s32[2]{0:T(128)} %blocks.1, bf16[2,512,256]{2,1,0:T(8,128)(2,1)} %prefix.1, s32[2,128]{1,0:T(2,128)} %bitcast.2, bf16[256,16,256]{2,1,0:T(8,128)(2,1)} %pool.1), custom_call_target="tpu_custom_call" | custom-call | tf_op jit(solution)/shard_map/pallas_call | solution.py:461
  61.2 1.6 %copy.9 = bf16[128,640]{1,0:T(8,128)(2,1)} copy(bf16[128,640]{1,0:T(8,128)(2,1)} %shard_map.73) | data formatting | bytes 327680

commit v6 on v5

--- a/solution.py
+++ b/solution.py
@@ -32,35 +32,34 @@
     ),
     (
         1040, 1041, 1552, 1553, 1296, 1297, 1808, 1809, 2576, 2577, 522, 515, 880, 881, 2064, 2065, 496, 497,
-        18, 19, 304, 305, 816, 817, 2320, 2321, 2832, 2833, 3088, 3089, 3600, 3601, 258, 267, 3344, 3345,
-        3856, 3857,
-    ),
-    (
-        1539, 1546, 1521, 786, 787, 1520, 2570, 2563, 848, 849, 1329, 2066, 2067, 464, 465, 20, 21, 336,
-        337, 2928, 2929, 2864, 2865, 882, 883, 2544, 2545, 2352, 2353, 818, 819, 490,
-    ),
-    (
-        2315, 483, 2306, 2896, 2897, 3594, 3587, 298, 850, 851, 1328, 291, 2834, 2835, 789, 788, 2068, 2069,
-        432, 6, 15, 433, 368, 369, 2512, 2513, 2384, 2385, 450, 2538, 2930, 2931, 2866, 2867, 885, 884,
-        821, 820, 459,
-    ),
-    (
-        2346, 2531, 3568, 3569, 3376, 3377, 2898, 2899, 853, 852, 2339, 2054, 2063, 400, 401, 1043, 322, 331,
-        1042, 1905, 1904, 2836, 2837, 783, 774, 1841, 1282, 1840, 2480, 2481, 2416, 2417, 419, 426, 362, 355,
-        1514, 1507, 1322, 2498, 2507, 2932, 2933, 2868, 2869, 878, 871, 814, 807, 1873, 1872, 2900, 2901, 847,
-        838, 1811, 2831, 1810, 2448, 2449, 386, 395, 2822, 1315, 1291, 2379, 3090, 3091, 1045, 1489, 1488, 1044,
-        1361, 1360, 2370, 2474, 2467, 2926, 2919, 2410, 2862, 3330, 2855, 2403, 3562, 3952, 3953, 3888, 3889, 1906,
-        1907, 1842, 1843, 3370, 3555, 2895, 2886, 2443, 2434,
-    ),
-    (
-        3920, 3921, 1874, 1875, 3092, 3093, 1030, 1039, 1456, 1457, 1392, 1393, 3536, 3537, 3408, 3409, 3858, 3859,
-        1474, 1483, 1355, 1346, 1812, 1813, 3363, 3339, 3954, 3955, 3890, 3891, 1908, 1909, 1844, 1845, 3922, 3923,
-        1876, 1877, 3078, 3087, 1424, 1425,
-    ),
-    (
-        3504, 3505, 3440, 3441, 3860, 3861, 1450, 1443, 1386, 1379, 1798, 1807, 3531, 3522, 3403, 3394, 3956, 3957,
-        3892, 3893, 1902, 1895, 1838, 1831, 3472, 3473, 1410, 1419, 3924, 3925, 1862, 1871, 3498, 3855, 3491, 3846,
-        3434, 3427, 3950, 3943, 3886, 3467, 3879, 3458, 3919, 3910,
+        18, 19, 304, 305, 816, 817, 2320, 2321, 2832, 2833, 3088, 3089, 3600, 3601, 258, 786, 787,
+    ),
+    (
+        267, 3344, 3345, 3856, 3857, 1539, 1546, 1521, 1520, 1329, 1328, 2570, 2563, 848, 849, 1291, 1042, 1043,
+        2066, 2067, 464, 465, 20, 21, 336, 337,
+    ),
+    (
+        2928, 2929, 2864, 2865, 882, 883, 2544, 2545, 2352, 2353, 818, 819, 490, 483, 2315, 2306, 2834, 2835,
+        3594, 3587, 298, 291, 2896, 2897, 850, 851, 3568, 3569, 3376, 3377, 3339, 788, 789, 3090, 3091, 1488,
+        1360, 1489, 1905, 2068, 2069, 432, 433, 6, 15, 368, 1904, 369, 2512, 2513, 2384, 2385, 450, 2538,
+        459, 2930, 2931, 2866, 2867, 885, 884, 821, 820, 2531, 2346, 331, 322,
+    ),
+    (
+        2898, 2899, 853, 852, 2339, 1361, 1841, 2836, 2837, 783, 774, 1840, 1873, 1872, 2054, 2063, 400, 401,
+        1045, 1044, 1811, 1282, 2480, 2481, 2416, 2417, 426, 419, 362, 355, 1514, 1810, 1507, 2507, 1315, 2498,
+        1322, 2932, 2933, 2868, 2869, 878, 871, 814, 807, 2379, 2370, 3536, 3537, 3408, 3409, 1474, 1346, 1483,
+        1355, 2900, 2901, 847, 838, 2831, 2822, 3952, 3953, 3888, 3889, 1906, 1907, 1842, 1843, 2448, 2449, 386,
+        395, 3920, 3921, 1874, 1875, 2474, 3092, 3093, 1457, 1456, 1030, 1039, 1393, 1392, 2467, 2410, 2926, 2919,
+        3330, 2862, 3562, 2403, 3522, 2855, 3555, 3858, 3859, 1812, 1813, 3394, 2895, 3363, 3370, 3531, 2886, 3403,
+        2443, 3954, 3955, 3890, 3891, 1908, 1909, 1844, 1845, 2434,
+    ),
+    (
+        3922, 3923, 1876, 1877, 3078, 3087, 1424, 1425, 3504, 3505, 3440, 3441, 1450, 1443, 1386, 1379, 3860, 3861,
+        1798, 1807, 3956, 3957, 3892, 3893, 1902, 1895, 1838, 1831,
+    ),
+    (
+        3472, 3473, 1410, 1419, 3498, 3924, 3925, 1862, 1871, 3491, 3434, 3427, 3855, 3846, 3950, 3943, 3886, 3467,
+        3458, 3879, 3910, 3919,
     ),
 )
 PIECES = ((0, 48), (48, 32), (0, 80))
@@ -191,20 +190,13 @@
     for part, width in ((qx, QX), (qz, QZ), (kx, KX), (vz, VZ)):
         part[z * NX + x] = w[:, start : start + width]
         start += width
-    def build_in():
-        for i in range(2 * REPEAT):
-            target = iota((N_ROLL, N_ROLL * TILE), 0) * TILE + i
-            pick_in[i * N_ROLL : (i + 1) * N_ROLL, :] = onehot(iota((N_ROLL, N_ROLL * TILE), 1) == target)
-
-    def build_out():
-        for i in range(2 * REPEAT):
-            lane = iota((N_ROLL * TILE, ROWS), 1) + (i % REPEAT) * ROWS
-            row = lax.shift_right_logical(lane, 6) if i < REPEAT else 2 * REPEAT
-            target = jnp.bitwise_and(lane, N_ROLL - 1) * TILE + row
-            pick_out[:, i * ROWS : (i + 1) * ROWS] = onehot(iota((N_ROLL * TILE, ROWS), 0) == target)
-
-    build_in()
-    build_out()
+    def build_blocks():
+        across = (jnp.bitwise_and(iota((256, 256), 0), 15) * TILE + lax.shift_right_logical(iota((256, 256), 0), 4))
+        down = (jnp.bitwise_and(iota((256, 256), 1), 15) * TILE + lax.shift_right_logical(iota((256, 256), 1), 4))
+        pick_in[...] = onehot(iota((256, 256), 1) == across)
+        pick_out[...] = onehot(iota((256, 256), 0) == down)
+
+    build_blocks()
     q_recv[...] = jnp.zeros_like(q_recv)
     o_recv[...] = jnp.zeros_like(o_recv)
     pl.semaphore_wait(barrier, len(peers))
@@ -386,12 +378,17 @@
     load_prefix.wait()
     all_of(q_recv, 10, r_q)
     came = q_recv[...].reshape(N_ROLL * TILE, HD)
-    outs, marks = [], []
     per = REPEAT * N_ROLL
+    part = REPEAT * TILE
+    turned = [
+        jnp.dot(
+            pick_in[: 2 * part, :], came[b * 256 : (b + 1) * 256], preferred_element_type=jnp.float32
+        ).astype(jnp.bfloat16)
+        for b in range(4)
+    ]
+    outs, marks = [], [jnp.zeros((TILE, HD), jnp.float32)] * 4
     for j in range(2):
-        queries = jnp.dot(
-            pick_in[j * per : (j + 1) * per, :], came, preferred_element_type=jnp.float32
-        ).astype(jnp.bfloat16)
+        queries = jnp.concatenate([q[j * part : (j + 1) * part] for q in turned], axis=0)
         scores = lax.dot_general(
             queries, pref[j, :, :HD], (((1,), (1,)), ((), ())), preferred_element_type=jnp.float32
         ) * SCALE
@@ -406,14 +403,22 @@
         hi = lse.astype(jnp.bfloat16).astype(jnp.float32)
         mid = (lse - hi).astype(jnp.bfloat16).astype(jnp.float32)
         low = lse - hi - mid
-        lane = iota((per, HD), 1)
-        first = (lax.shift_right_logical(iota((per, HD), 0), 6) + j * REPEAT) * 3
-        mark = jnp.where(lane == first, hi, jnp.where(lane == first + 1, mid, jnp.where(lane == first + 2, low, 0.0)))
-        marks.append(mark.astype(jnp.bfloat16))
-    stacked = jnp.concatenate(outs + marks, axis=0)
-    o_send[...] = jnp.dot(pick_out[...], stacked, preferred_element_type=jnp.float32).astype(
-        jnp.bfloat16
-    ).reshape(N_ROLL, TILE, HD)
+        lane = iota((TILE, HD), 1)
+        for b in range(4):
+            for h in range(REPEAT):
+                first = (j * REPEAT + h) * 3
+                at = slice(b * part + h * TILE, b * part + (h + 1) * TILE)
+                marks[b] = jnp.where(
+                    lane == first, hi[at], jnp.where(lane == first + 1, mid[at], jnp.where(lane == first + 2, low[at], marks[b]))
+                )
+    for b in range(4):
+        rows = slice(b * part, (b + 1) * part)
+        stacked = jnp.concatenate(
+            [outs[0][rows], outs[1][rows], marks[b].astype(jnp.bfloat16), jnp.zeros((5 * TILE, HD), jnp.bfloat16)], axis=0
+        )
+        o_send[b * TILE : (b + 1) * TILE] = jnp.dot(
+            pick_out[...], stacked, preferred_element_type=jnp.float32
+        ).astype(jnp.bfloat16).reshape(TILE, TILE, HD)
     exchange(o_send, o_recv, 12, s_o, r_o)
     total_of(5, 2, r_c.at[1])
     lax.fori_loop(0, ROWS // SB, local_block, 0)
@@ -480,8 +485,8 @@
             pltpu.VMEM(prefix_kv.shape, bf16),
             pltpu.VMEM(suffix_pool.shape, bf16),
             pltpu.VMEM((N_ROLL * TILE, REPEAT * ROWS), bf16),
-            pltpu.VMEM((2 * REPEAT * N_ROLL, N_ROLL * TILE), bf16),
-            pltpu.VMEM((N_ROLL * TILE, 2 * REPEAT * ROWS), bf16),
+            pltpu.VMEM((256, 256), bf16),
+            pltpu.VMEM((256, 256), bf16),
             pltpu.VMEM(((REPEAT + 1) * ROWS, N_ROLL * TILE), bf16),
             tiles, tiles, tiles, tiles,
             pltpu.VMEM((REPEAT, ROWS, HD), f32),

time: 62.9 us -> 60.2 us (0.957)
  Pallas kernels: 61.2 us -> 58.4 us
    pallas_call x1, Pallas kernels: 61.2 us -> 58.4 us  [per_device(): pl.pallas_call(attend_kernel, out_shape=jax.ShapeDtypeStruct((ROWS, REPEA...]
where the time goes in v6:
time: 60.2 us; the launch traced here: 60 us
  Pallas kernels  58.4 us (97%)
  local copies, waits for them, and re-layouts  1.6 us (3%)
    pallas_call x1, Pallas kernels, per_device(): pl.pallas_call(attend_kernel, out_shape=jax.ShapeDtypeStruct((ROWS, REPEA...  58.4 us
    unnamed x1, local copies, waits for them, and re-layouts  1.6 us

profile of v6, /device:TPU:8, one launch (start us, length us, event | category | flops | bytes accessed | tf_op | source)
XLA Modules:
  0.0 60.0 jit_solution(15542648113592413871)
XLA Ops:
  0.0 58.4 %shard_map.73 = bf16[128,640]{1,0:T(8,128)(2,1)} custom-call(bf16[128,1280]{1,0:T(8,128)(2,1)} %hidden_hbm.1, bf16[80,896]{1,0:T(8,128)(2,1)} %w_hbm.1, s32[1,128]{1,0:T(1,128)} %bitcast.3, s32[2]{0:T(128)} %blocks.1, bf16[2,512,256]{2,1,0:T(8,128)(2,1)} %prefix.1, s32[2,128]{1,0:T(2,128)} %bitcast.2, bf16[256,16,256]{2,1,0:T(8,128)(2,1)} %pool.1), custom_call_target="tpu_custom_call" | custom-call | tf_op jit(solution)/shard_map/pallas_call | solution.py:466
  58.4 1.6 %copy.9 = bf16[128,640]{1,0:T(8,128)(2,1)} copy(bf16[128,640]{1,0:T(8,128)(2,1)} %shard_map.73) | data formatting | bytes 327680

commit v7 on v6

--- a/solution.py
+++ b/solution.py
@@ -154,7 +154,7 @@
 
 def attend_kernel(
     hidden_hbm, w_hbm, group_hbm, blocks, prefix, table_hbm, pool, out,
-    hidden, w, group, table,
+    hidden, w, group, table, result,
     qx, qz, kx, vz, ab, nb, ssq_s, ssq_r, cs, cb, cr,
     un, pref, pages, pick_send, pick_in, pick_out, pick_home,
     q_send, q_recv, o_send, o_recv, local_out, local_lse, gathered,
@@ -221,21 +221,15 @@
         send(ssq_s, ssq_r.at[k], s_ss, r_ss, me.other(False, tp))
     load_group.wait()
     load_table.wait()
-    slot = lax.shift_right_logical(group[...], 1) * TILE + jnp.bitwise_and(group[...], 1) * REPEAT
-    slot_rows = jnp.broadcast_to(slot, (ROWS, ROWS)).T
     group_rows = jnp.broadcast_to(group[...], (ROWS, ROWS)).T
 
-    def build_send():
-        for h in range(REPEAT):
-            pick_send[:, h * ROWS : (h + 1) * ROWS] = onehot(iota((N_ROLL * TILE, ROWS), 0) == slot + h)
-
-    def build_home():
-        for b in range(N_ROLL * TILE // ROWS):
-            column = iota((ROWS, ROWS), 1) + b * ROWS
-            for h in range(REPEAT):
-                pick_home[h * ROWS : (h + 1) * ROWS, b * ROWS : (b + 1) * ROWS] = onehot(column == slot_rows + h)
-            target = lax.shift_right_logical(group_rows, 1) * TILE + 2 * REPEAT
-            pick_home[REPEAT * ROWS :, b * ROWS : (b + 1) * ROWS] = onehot(column == target)
+    def build_picks():
+        shape = (ROWS, ROWS)
+        down = jnp.bitwise_and(iota(shape, 0), N_ROLL - 1) * 2 + lax.shift_right_logical(iota(shape, 0), 6)
+        across = jnp.bitwise_and(iota(shape, 1), N_ROLL - 1) * 2 + lax.shift_right_logical(iota(shape, 1), 6)
+        pick_send[...] = onehot(group[...] == down)
+        pick_home[:, :ROWS] = onehot(group_rows == across)
+        pick_home[:, ROWS:] = onehot(lax.shift_right_logical(group_rows, 1) == iota(shape, 1))
 
     def gather_pages():
         load_pages.wait()
@@ -303,7 +297,7 @@
     run(1)
     run(2)
     run(3)
-    build_send()
+    build_picks()
     pass_rows()
     run(4)
     g1.finish()
@@ -311,15 +305,21 @@
     product(3, qz, 0, 256, r_c.at[0])
     product(0, qx, 0, 256, r_c.at[0])
     product(2, qx, 256, 128, r_c.at[0])
-    build_home()
-    gather_pages()
     run(5)
     total_of(0, 5, r_c.at[0])
 
-    rows = jnp.concatenate([un[:, h * HD : (h + 1) * HD] for h in range(REPEAT)], axis=0)
-    q_send[...] = jnp.dot(pick_send[...], rows, preferred_element_type=jnp.float32).astype(
-        jnp.bfloat16
-    ).reshape(N_ROLL, TILE, HD)
+    by_owner = jnp.dot(
+        pick_send[...], un[:, : REPEAT * HD], preferred_element_type=jnp.float32
+    ).astype(jnp.bfloat16)
+    for b in range(4):
+        parts = [
+            by_owner[j * N_ROLL + b * TILE : j * N_ROLL + (b + 1) * TILE, h * HD : (h + 1) * HD]
+            for j in range(2) for h in range(REPEAT)
+        ]
+        stacked = jnp.concatenate(parts + [jnp.zeros((6 * TILE, HD), jnp.bfloat16)], axis=0)
+        q_send[b * TILE : (b + 1) * TILE] = jnp.dot(
+            pick_out[...], stacked, preferred_element_type=jnp.float32
+        ).astype(jnp.bfloat16).reshape(TILE, TILE, HD)
 
     def exchange(src, dst, rows, s_sem, r_sem):
         here = y * NX + x
@@ -342,6 +342,7 @@
 
     exchange(q_send, q_recv, 10, s_q, r_q)
     run(6)
+    gather_pages()
     g2.finish()
     product(5, kx, 0, 128, r_c.at[1])
     product(6, vz, 0, 128, r_c.at[1])
@@ -423,10 +424,26 @@
     total_of(5, 2, r_c.at[1])
     lax.fori_loop(0, ROWS // SB, local_block, 0)
     all_of(o_recv, 12, r_o)
+    came = o_recv[...].reshape(N_ROLL * TILE, HD)
+    turned = [
+        jnp.dot(
+            pick_in[: 11 * TILE, :], came[b * 256 : (b + 1) * 256], preferred_element_type=jnp.float32
+        ).astype(jnp.bfloat16)
+        for b in range(4)
+    ]
+    by_head = [
+        jnp.concatenate(
+            [turned[b][(j * REPEAT + h) * TILE : (j * REPEAT + h + 1) * TILE] for j in range(2) for b in range(4)], axis=0
+        )
+        for h in range(REPEAT)
+    ]
+    marks = [turned[b][10 * TILE : 11 * TILE] for b in range(4)] + [jnp.zeros((N_ROLL, HD), jnp.bfloat16)]
+    terms = jnp.dot(
+        pick_home[:, ROWS:], jnp.concatenate(marks, axis=0), preferred_element_type=jnp.float32
+    )
     back = jnp.dot(
-        pick_home[...], o_recv[...].reshape(N_ROLL * TILE, HD), preferred_element_type=jnp.float32
+        pick_home[:, :ROWS], jnp.concatenate(by_head, axis=1), preferred_element_type=jnp.float32
     )
-    terms = back[REPEAT * ROWS :]
     second = jnp.bitwise_and(group_rows, 1) * REPEAT
     lane = iota((ROWS, HD), 1)
     for h in range(REPEAT):
@@ -437,9 +454,12 @@
         top = jnp.maximum(p_lse, l_lse)
         ep = jnp.exp(p_lse - top)
         el = jnp.exp(l_lse - top)
-        mixed = (ep * back[h * ROWS : (h + 1) * ROWS] + el * local_out[h]) / (ep + el)
-        out[:, h * HD : (h + 1) * HD] = mixed.astype(jnp.bfloat16)
-
+        mixed = (ep * back[:, h * HD : (h + 1) * HD] + el * local_out[h]) / (ep + el)
+        cols = slice(h * HD, (h + 1) * HD)
+        result[:, cols] = mixed.astype(jnp.bfloat16)
+        pltpu.make_async_copy(result.at[:, cols], out.at[:, cols], load_sem.at[6]).start()
+
+    arrived(result, load_sem.at[6])
     all_of(q_send, 10, s_q)
     all_of(o_send, 12, s_o)
     g1.sent()
@@ -467,12 +487,13 @@
         attend_kernel,
         out_shape=jax.ShapeDtypeStruct((ROWS, REPEAT * HD), bf16),
         in_specs=[hbm, hbm, hbm, smem, hbm, hbm, hbm],
-        out_specs=vmem,
+        out_specs=hbm,
         scratch_shapes=[
             pltpu.VMEM((ROWS, 10 * HD), bf16),
             pltpu.VMEM((SHARD, QX + QZ + KX + VZ), bf16),
             pltpu.VMEM((1, ROWS), jnp.int32),
             pltpu.SMEM((SPAGES, ROWS), jnp.int32),
+            pltpu.VMEM((ROWS, REPEAT * HD), bf16),
             *(pltpu.VMEM((NZ * NX, SHARD, width), bf16) for width in (QX, QZ, KX, VZ)),
             pltpu.VMEM((8, ROWS, 640), bf16),
             pltpu.VMEM((2, ROWS, 640), bf16),
@@ -484,16 +505,16 @@
             pltpu.VMEM((ROWS, QX + QZ + KX + VZ), bf16),
             pltpu.VMEM(prefix_kv.shape, bf16),
             pltpu.VMEM(suffix_pool.shape, bf16),
-            pltpu.VMEM((N_ROLL * TILE, REPEAT * ROWS), bf16),
+            pltpu.VMEM((ROWS, ROWS), bf16),
             pltpu.VMEM((256, 256), bf16),
             pltpu.VMEM((256, 256), bf16),
-            pltpu.VMEM(((REPEAT + 1) * ROWS, N_ROLL * TILE), bf16),
+            pltpu.VMEM((ROWS, 2 * ROWS), bf16),
             tiles, tiles, tiles, tiles,
             pltpu.VMEM((REPEAT, ROWS, HD), f32),
             pltpu.VMEM((REPEAT, ROWS, HD), f32),
             pltpu.VMEM((ROWS, SPAGES, PAGE, 2 * HD), bf16),
             *sems,
-            dma((6,)), dma, dma, dma, dma,
+            dma((7,)), dma, dma, dma, dma,
             *gather_sems,
         ],
         compiler_params=pltpu.CompilerParams(

time: 60.2 us -> 59.7 us (level)
  no operation moved by 1% of the time
where the time goes in v7:
time: 59.7 us; the launch traced here: 59.6 us
  Pallas kernels  58 us (97%)
  local copies, waits for them, and re-layouts  1.6 us (3%)
    pallas_call x1, Pallas kernels, per_device(): pl.pallas_call(attend_kernel, out_shape=jax.ShapeDtypeStruct((ROWS, REPEA...  58 us
    unnamed x1, local copies, waits for them, and re-layouts  1.6 us

profile of v7, /device:TPU:8, one launch (start us, length us, event | category | flops | bytes accessed | tf_op | source)
XLA Modules:
  0.0 59.6 jit_solution(4059726402174207734)
XLA Ops:
  0.0 58.0 %shard_map.73 = bf16[128,640]{1,0:T(8,128)(2,1)} custom-call(bf16[128,1280]{1,0:T(8,128)(2,1)} %hidden_hbm.1, bf16[80,896]{1,0:T(8,128)(2,1)} %w_hbm.1, s32[1,128]{1,0:T(1,128)} %bitcast.3, s32[2]{0:T(128)} %blocks.1, bf16[2,512,256]{2,1,0:T(8,128)(2,1)} %prefix.1, s32[2,128]{1,0:T(2,128)} %bitcast.2, bf16[256,16,256]{2,1,0:T(8,128)(2,1)} %pool.1), custom_call_target="tpu_custom_call" | custom-call | tf_op jit(solution)/shard_map/pallas_call | solution.py:486
  58.0 1.6 %copy.9 = bf16[128,640]{1,0:T(8,128)(2,1)} copy(bf16[128,640]{1,0:T(8,128)(2,1)} %shard_map.73) | data formatting | bytes 327680

commit v8 on v7

--- a/solution.py
+++ b/solution.py
@@ -302,9 +302,9 @@
     run(4)
     g1.finish()
     arrived(ab.at[pl.ds(0, 4)], r_b)
+    product(2, qx, 256, 128, r_c.at[0])
     product(3, qz, 0, 256, r_c.at[0])
     product(0, qx, 0, 256, r_c.at[0])
-    product(2, qx, 256, 128, r_c.at[0])
     run(5)
     total_of(0, 5, r_c.at[0])
 

time: 59.7 us -> 59.6 us (level)
  no operation moved by 1% of the time
where the time goes in v8:
time: 59.6 us; the launch traced here: 59.5 us
  Pallas kernels  57.9 us (97%)
  local copies, waits for them, and re-layouts  1.6 us (3%)
    pallas_call x1, Pallas kernels, per_device(): pl.pallas_call(attend_kernel, out_shape=jax.ShapeDtypeStruct((ROWS, REPEA...  57.9 us
    unnamed x1, local copies, waits for them, and re-layouts  1.6 us

profile of v8, /device:TPU:8, one launch (start us, length us, event | category | flops | bytes accessed | tf_op | source)
XLA Modules:
  0.0 59.5 jit_solution(17853551649600573039)
XLA Ops:
  0.0 57.9 %shard_map.73 = bf16[128,640]{1,0:T(8,128)(2,1)} custom-call(bf16[128,1280]{1,0:T(8,128)(2,1)} %hidden_hbm.1, bf16[80,896]{1,0:T(8,128)(2,1)} %w_hbm.1, s32[1,128]{1,0:T(1,128)} %bitcast.3, s32[2]{0:T(128)} %blocks.1, bf16[2,512,256]{2,1,0:T(8,128)(2,1)} %prefix.1, s32[2,128]{1,0:T(2,128)} %bitcast.2, bf16[256,16,256]{2,1,0:T(8,128)(2,1)} %pool.1), custom_call_target="tpu_custom_call" | custom-call | tf_op jit(solution)/shard_map/pallas_call | solution.py:486
  57.9 1.6 %copy.9 = bf16[128,640]{1,0:T(8,128)(2,1)} copy(bf16[128,640]{1,0:T(8,128)(2,1)} %shard_map.73) | data formatting | bytes 327680
